TPU v7x, 32 devices: a whole 2x2x4 slice. The times are simulated.
32 devices in a mesh: rows: 8 (over z, y), vecs: 4 (over x, core).
Axes of the slice: x: 2, y: 2, z: 4, core: 2. Of those that a mesh axis runs over, the one named last changes fastest.
Arguments:
- vectors: bfloat16 [32768, 1024], P('rows', 'vecs'), may hold values from -6 to 6, as said below
- blocks: bfloat16 [256, 5, 128, 128], P('rows'), may hold values from -0.25 to 0.25
- columns: int32 [256, 5], P('rows'), may hold values from 0 to 255, as said below
Outputs:
- basis: float32 [32768, 1024], P('rows', 'vecs')
Inputs may be any that keep to these rules, and one draw needn't show every extreme that they name: Each block row i names 5 block columns of the form i + d clipped to 0 .. 255, with distinct d in -8 .. 8; near the grid's ends some may repeat. `vectors`: entries of order one.
All inputs are finite; a program needn't handle non-finite values.
Results may differ from a plain program's by a relative error of at most 0.0075.
Values may be sent and summed in bfloat16 or wider, within the bound.
A program may use at most 128 MiB of HBM per device.

v0:
```python
import jax
import jax.numpy as jnp
from jax import lax
from jax.sharding import PartitionSpec as P

DEGREE = 4


filter_center = 0.25
filter_radius = 1.25


def with_halo(shard, sides, width):
    for axis, dim in sides:
        count, length = (lax.axis_size(axis), shard.shape[dim])
        up = [(i, (i + 1) % count) for i in range(count - 1)]
        down = [(j, i) for i, j in up]
        last = lax.slice_in_dim(shard, length - width, length, axis=dim)
        first = lax.slice_in_dim(shard, 0, width, axis=dim)
        before = lax.ppermute(last, axis, up)
        after = lax.ppermute(first, axis, down)
        shard = jnp.concatenate([before, shard, after], axis=dim)
    return shard


def product(vec_bf, blocks, local_index):
    block_rows = blocks.shape[0]
    size_b = blocks.shape[2]
    width = vec_bf.shape[1]
    reach = block_rows // 4
    padded = with_halo(vec_bf, (("rows", 0),), reach * size_b)
    stacked = padded.reshape(block_rows + 2 * reach, size_b, width)
    picked = stacked[local_index]
    result = jnp.einsum("rjab,rjbk->rak", blocks, picked, preferred_element_type=jnp.float32)
    return result.reshape(block_rows * size_b, width)


def split_apply(left_bf, factor):
    factor_high = factor.astype(jnp.bfloat16)
    factor_low = (factor - factor_high.astype(jnp.float32)).astype(jnp.bfloat16)
    first = jnp.dot(left_bf, factor_high.T, preferred_element_type=jnp.float32)
    second = jnp.dot(left_bf, factor_low.T, preferred_element_type=jnp.float32)
    return first + second


def shards(vectors, blocks, columns):
    block_rows = blocks.shape[0]
    reach = block_rows // 4
    first_row = lax.axis_index("rows") * block_rows
    local_index = columns - first_row + reach
    total_rows = vectors.shape[0] * lax.axis_size("rows")
    older = vectors.astype(jnp.float32)
    current = (product(vectors, blocks, local_index) - filter_center * older) / filter_radius
    for iteration in range(1, DEGREE):
        rounded = current.astype(jnp.bfloat16)
        newer = (
            2.0 * (product(rounded, blocks, local_index) - filter_center * current) / filter_radius
            - older
        )
        older = current
        current = newer
    final = current.astype(jnp.bfloat16)
    panel_width = final.shape[1]
    full_width = panel_width * lax.axis_size("vecs")
    identity = jnp.eye(full_width, dtype=jnp.float32)
    whole_block = lax.all_gather(final, "vecs", axis=1, tiled=True)
    panel = jnp.dot(final.T, whole_block, preferred_element_type=jnp.float32)
    summed = lax.psum(panel, "rows")
    gram_matrix = lax.all_gather(summed, "vecs", axis=0, tiled=True) / total_rows
    lower = jnp.linalg.cholesky(gram_matrix)
    inverse = lax.linalg.triangular_solve(lower, identity, left_side=True, lower=True)
    own_rows = lax.dynamic_slice_in_dim(
        inverse, lax.axis_index("vecs") * panel_width, panel_width, 0
    )
    return split_apply(whole_block, own_rows)


def solution(mesh):
    in_specs = (P("rows", "vecs"), P("rows", None, None, None), P("rows", None))
    out_specs = P("rows", "vecs")
    return jax.shard_map(shards, mesh=mesh, in_specs=in_specs, out_specs=out_specs, check_vma=False)
```

profile of v0, /device:TPU:0, one launch (start us, length us, event | category | flops | bytes accessed | tf_op | source)
XLA Modules:
  0.0 754.6 jit_solution(8515104857736990841)
XLA Ops:
  7.8 4.9 collective-permute-start
  15.0 20.2 %collective-permute-done = bf16[1024,256]{1,0:T(8,128)(2,1)S(1)} collective-permute-done((bf16[1024,256]{1,0:T(8,128)(2,1)S(1)}, bf16[1024,256]{1,0:T(8,128)(2,1)S(1)}, u32[]{:S(2)}, u32[]{:S(2)}) %collective-permute-start) | collective-permute-done | bytes 524320 | tf_op jit(solution)/shard_map/ppermute | solution.py:20
  38.0 7.6 %gather_fusion = bf16[160,128,256]{2,1,0:T(8,128)(2,1)} fusion(bf16[48,128,256]{2,1,0:T(8,128)(2,1)S(1)} %bitcast.196, s32[1024]{0:T(1024)S(1)} %pad_clamp_fusion), kind=kCustom, calls=%fused_computation | custom fusion | bytes 20972160 | tf_op jit(solution)/shard_map/gather | solution.py:33
  45.6 7.5 fusion.88
  55.3 4.4 collective-permute-start.2
  61.0 20.2 %collective-permute-done.2 = bf16[1024,256]{1,0:T(8,128)(2,1)S(1)} collective-permute-done((bf16[1024,256]{1,0:T(8,128)(2,1)S(1)}, bf16[1024,256]{1,0:T(8,128)(2,1)S(1)}, u32[]{:S(2)}, u32[]{:S(2)}) %collective-permute-start.2) | collective-permute-done | bytes 524320 | tf_op jit(solution)/shard_map/ppermute | solution.py:20
  83.1 9.5 %gather_fusion.1 = bf16[160,128,256]{2,1,0:T(8,128)(2,1)} fusion(bf16[48,128,256]{2,1,0:T(8,128)(2,1)} %bitcast.194, s32[1024]{0:T(1024)S(1)} %pad_clamp_fusion), kind=kCustom, calls=%fused_computation.1 | custom fusion | bytes 20972160 | tf_op jit(solution)/shard_map/gather | solution.py:33
  92.6 7.5 fusion.89
  102.3 4.4 collective-permute-start.4
  108.5 18.9 %collective-permute-done.4 = bf16[1024,256]{1,0:T(8,128)(2,1)S(1)} collective-permute-done((bf16[1024,256]{1,0:T(8,128)(2,1)S(1)}, bf16[1024,256]{1,0:T(8,128)(2,1)S(1)}, u32[]{:S(2)}, u32[]{:S(2)}) %collective-permute-start.4) | collective-permute-done | bytes 524320 | tf_op jit(solution)/shard_map/ppermute | solution.py:20
  129.1 9.5 %gather_fusion.2 = bf16[160,128,256]{2,1,0:T(8,128)(2,1)} fusion(bf16[48,128,256]{2,1,0:T(8,128)(2,1)} %bitcast.195, s32[1024]{0:T(1024)S(1)} %pad_clamp_fusion), kind=kCustom, calls=%fused_computation.2 | custom fusion | bytes 20972160 | tf_op jit(solution)/shard_map/gather | solution.py:33
  138.6 7.5 fusion.90
  146.6 2.6 fusion.80
  149.3 4.4 collective-permute-start.6
  155.1 7.3 collective-permute-done.6
  162.3 11.6 %collective-permute-done.7 = bf16[1024,256]{1,0:T(8,128)(2,1)S(1)} collective-permute-done((bf16[1024,256]{1,0:T(8,128)(2,1)S(1)}, bf16[1024,256]{1,0:T(8,128)(2,1)S(1)}, u32[]{:S(2)}, u32[]{:S(2)}) %collective-permute-start.7) | collective-permute-done | bytes 524320 | tf_op jit(solution)/shard_map/ppermute | solution.py:21
  175.8 9.5 %gather_fusion.3 = bf16[160,128,256]{2,1,0:T(8,128)(2,1)} fusion(bf16[48,128,256]{2,1,0:T(8,128)(2,1)} %bitcast.193, s32[1024]{0:T(1024)S(1)} %pad_clamp_fusion), kind=kCustom, calls=%fused_computation.3 | custom fusion | bytes 20972160 | tf_op jit(solution)/shard_map/gather | solution.py:33
  185.3 7.5 fusion.91
  194.5 4.4 fusion.3
  198.9 68.9 %all-gather.3.cloned.1.call-done = bf16[4096,1024]{1,0:T(8,128)(2,1)} async-done(((bf16[4096,256]{1,0:T(8,128)(2,1)}), bf16[4096,1024]{1,0:T(8,128)(2,1)}) %all-gather.3.cloned.1.call-update) | async-done | bytes 8388624 | tf_op jit(solution)/shard_map/all_gather | solution.py:66
  267.9 8.4 %fusion.87 = f32[256,1024]{0,1:T(8,128)} fusion(bf16[4096,256]{1,0:T(8,128)(2,1)} %fusion.3, bf16[4096,1024]{1,0:T(8,128)(2,1)} %all-gather.3.cloned.1.call-done), kind=kOutput, calls=%fused_computation.195 | convolution fusion | flops 2147483648 | bytes 11534336 | tf_op jit(solution)/shard_map/dot_general | solution.py:67
  276.4 78.3 %all-reduce.3.cloned.1.call-done = f32[256,1024]{0,1:T(8,128)} async-done(((f32[256,1024]{0,1:T(8,128)}), f32[256,1024]{0,1:T(8,128)}) %all-reduce.3.cloned.1.call-update) | async-done | bytes 1048592 | tf_op jit(solution)/shard_map/psum | solution.py:68
  357.6 32.8 %all-gather.5.cloned.1.call-done = f32[1024,1024]{0,1:T(8,128)} async-done(((f32[256,1024]{0,1:T(8,128)}), f32[1024,1024]{0,1:T(8,128)}) %all-gather.5.cloned.1.call-update) | async-done | bytes 4194320 | tf_op jit(solution)/shard_map/all_gather | solution.py:69
  390.4 5.0 broadcast_multiply_fusion
  395.4 5.5 copy.8
  400.9 4.4 fusion.7
  407.3 11.7 %cholesky.223 = f32[128,128]{1,0:T(8,128)S(1)} custom-call(f32[128,128]{1,0:T(8,128)S(1)} %cholesky.580), custom_call_target="Cholesky" | custom-call | tf_op jit(solution)/shard_map/jit(cholesky)/cholesky | solution.py:70
  419.1 9.8 %custom-call.62 = f32[1,128,128]{1,2,0:T(8,128)S(1)} custom-call(f32[1,128,128]{2,1,0:T(8,128)S(1)} %get-tuple-element.77), custom_call_target="InvertDiagBlocksLowerTriangular" | custom-call | tf_op jit(solution)/shard_map/jit(cholesky)/cholesky | solution.py:70
  435.3 11.9 %cholesky.244 = f32[128,128]{1,0:T(8,128)S(1)} custom-call(f32[128,128]{1,0:T(8,128)S(1)} %cholesky.584), custom_call_target="Cholesky" | custom-call | tf_op jit(solution)/shard_map/jit(cholesky)/cholesky | solution.py:70
  447.8 9.8 %custom-call.63 = f32[1,128,128]{1,2,0:T(8,128)S(1)} custom-call(f32[1,128,128]{2,1,0:T(8,128)S(1)} %get-tuple-element.74), custom_call_target="InvertDiagBlocksLowerTriangular" | custom-call | tf_op jit(solution)/shard_map/jit(cholesky)/cholesky | solution.py:70
  461.0 11.7 %cholesky.468 = f32[128,128]{1,0:T(8,128)S(1)} custom-call(f32[128,128]{1,0:T(8,128)S(1)} %cholesky.589), custom_call_target="Cholesky" | custom-call | tf_op jit(solution)/shard_map/jit(cholesky)/cholesky | solution.py:70
  474.0 9.8 %custom-call.64 = f32[1,128,128]{1,2,0:T(8,128)S(1)} custom-call(f32[1,128,128]{2,1,0:T(8,128)S(1)} %get-tuple-element.71), custom_call_target="InvertDiagBlocksLowerTriangular" | custom-call | tf_op jit(solution)/shard_map/jit(cholesky)/cholesky | solution.py:70
  487.3 12.1 %cholesky.487 = f32[128,128]{1,0:T(8,128)S(1)} custom-call(f32[128,128]{1,0:T(8,128)S(1)} %cholesky.594), custom_call_target="Cholesky" | custom-call | tf_op jit(solution)/shard_map/jit(cholesky)/cholesky | solution.py:70
  500.7 9.8 %custom-call.65 = f32[1,128,128]{1,2,0:T(8,128)S(1)} custom-call(f32[1,128,128]{2,1,0:T(8,128)S(1)} %get-tuple-element.68), custom_call_target="InvertDiagBlocksLowerTriangular" | custom-call | tf_op jit(solution)/shard_map/jit(cholesky)/cholesky | solution.py:70
  514.0 11.7 %cholesky.506 = f32[128,128]{1,0:T(8,128)S(1)} custom-call(f32[128,128]{1,0:T(8,128)S(1)} %cholesky.599), custom_call_target="Cholesky" | custom-call | tf_op jit(solution)/shard_map/jit(cholesky)/cholesky | solution.py:70
  526.9 10.0 %custom-call.66 = f32[1,128,128]{1,2,0:T(8,128)S(1)} custom-call(f32[1,128,128]{2,1,0:T(8,128)S(1)} %get-tuple-element.65), custom_call_target="InvertDiagBlocksLowerTriangular" | custom-call | tf_op jit(solution)/shard_map/jit(cholesky)/cholesky | solution.py:70
  540.2 11.7 %cholesky.526 = f32[128,128]{1,0:T(8,128)S(1)} custom-call(f32[128,128]{1,0:T(8,128)S(1)} %cholesky.604), custom_call_target="Cholesky" | custom-call | tf_op jit(solution)/shard_map/jit(cholesky)/cholesky | solution.py:70
  553.2 9.8 %custom-call.67 = f32[1,128,128]{1,2,0:T(8,128)S(1)} custom-call(f32[1,128,128]{2,1,0:T(8,128)S(1)} %get-tuple-element.62), custom_call_target="InvertDiagBlocksLowerTriangular" | custom-call | tf_op jit(solution)/shard_map/jit(cholesky)/cholesky | solution.py:70
  566.0 11.9 %cholesky.546 = f32[128,128]{1,0:T(8,128)S(1)} custom-call(f32[128,128]{1,0:T(8,128)S(1)} %cholesky.609), custom_call_target="Cholesky" | custom-call | tf_op jit(solution)/shard_map/jit(cholesky)/cholesky | solution.py:70
  579.2 9.8 %custom-call.68 = f32[1,128,128]{1,2,0:T(8,128)S(1)} custom-call(f32[1,128,128]{2,1,0:T(8,128)S(1)} %get-tuple-element.59), custom_call_target="InvertDiagBlocksLowerTriangular" | custom-call | tf_op jit(solution)/shard_map/jit(cholesky)/cholesky | solution.py:70
  591.7 11.7 %cholesky.564 = f32[128,128]{1,0:T(8,128)S(1)} custom-call(f32[128,128]{1,0:T(8,128)S(1)} %convolution_subtract_fusion.11), custom_call_target="Cholesky" | custom-call | tf_op jit(solution)/shard_map/jit(cholesky)/cholesky | solution.py:70
  610.4 4.9 select_select_fusion
  615.2 23.9 %while.1 = (s32[]{:T(128)}, f32[1024,1024]{1,0:T(8,128)}, s32[8,2]{0,1:T(2,128)S(1)}, f32[8,128,128]{2,1,0:T(8,128)S(1)}, s32[]{:T(128)}) while((s32[]{:T(128)}, f32[1024,1024]{1,0:T(8,128)}, s32[8,2]{0,1:T(2,128)S(1)}, f32[8,128,128]{2,1,0:T(8,128)S(1)}, s32[]{:T(128)}) %tuple.61), condition=%wide.while_cond, body=%wide.while_body.sunk | while | flops 2 | bytes 131189 | solution.py:71
  639.1 79.0 %custom-call.69 = f32[8,128,128]{1,2,0:T(8,128)S(1)} custom-call(f32[8,128,128]{2,1,0:T(8,128)S(1)} %get-tuple-element.12), custom_call_target="InvertDiagBlocksLowerTriangular" | custom-call | tf_op jit(solution)/shard_map/triangular_solve | solution.py:71
  729.5 2.8 convolution_subtract_fusion.2
  733.0 3.0 convolution_subtract_fusion.1
  736.7 3.4 convolution_subtract_fusion.3
  743.2 4.7 convolution_add_fusion
  (137 shorter events, 101.6 us)
Async XLA Ops:
  6.5 261.4 %all-gather.3.cloned.1.call-start = ((), (), s32[]{:S(2)}) async-start(), calls=%async_computation | async-start | bytes 10485760 | tf_op jit(solution)/shard_map/all_gather | solution.py:66
  7.8 27.3 %collective-permute-start = (bf16[1024,256]{1,0:T(8,128)(2,1)S(1)}, bf16[1024,256]{1,0:T(8,128)(2,1)S(1)}, u32[]{:S(2)}, u32[]{:S(2)}) collective-permute-start(bf16[1024,256]{1,0:T(8,128)(2,1)S(1)} %get-tuple-element.29), channel_id=1, source_target_pairs={{0,4},{4,8},{8,12},{12,16},{16,20},{20,24},{24,28},{1,5},{5,9},{9,... | collective-permute-start | bytes 1572872 | tf_op jit(solution)/shard_map/ppermute | solution.py:20
  12.7 23.2 %collective-permute-start.1 = (bf16[1024,256]{1,0:T(8,128)(2,1)S(1)}, bf16[1024,256]{1,0:T(8,128)(2,1)}, u32[]{:S(2)}, u32[]{:S(2)}) collective-permute-start(bf16[1024,256]{1,0:T(8,128)(2,1)S(1)} %get-tuple-element.30), channel_id=1, source_target_pairs={{4,0},{8,4},{12,8},{16,12},{20,16},{24,20},{28,24},{5,1},{9,5},{13... | collective-permute-start | bytes 1572872 | tf_op jit(solution)/shard_map/ppermute | solution.py:21
  35.1 0.8 copy-start.12
  45.6 7.5 copy-start.7
  53.2 2.0 copy-start
  55.3 25.9 %collective-permute-start.2 = (bf16[1024,256]{1,0:T(8,128)(2,1)S(1)}, bf16[1024,256]{1,0:T(8,128)(2,1)S(1)}, u32[]{:S(2)}, u32[]{:S(2)}) collective-permute-start(bf16[1024,256]{1,0:T(8,128)(2,1)S(1)} %get-tuple-element.27), channel_id=1, source_target_pairs={{0,4},{4,8},{8,12},{12,16},{16,20},{20,24},{24,28},{1,5},{5,9},{9,... | collective-permute-start | bytes 1572872 | tf_op jit(solution)/shard_map/ppermute | solution.py:20
  59.7 21.5 %collective-permute-start.3 = (bf16[1024,256]{1,0:T(8,128)(2,1)S(1)}, bf16[1024,256]{1,0:T(8,128)(2,1)S(1)}, u32[]{:S(2)}, u32[]{:S(2)}) collective-permute-start(bf16[1024,256]{1,0:T(8,128)(2,1)S(1)} %get-tuple-element.28), channel_id=1, source_target_pairs={{4,0},{8,4},{12,8},{16,12},{20,16},{24,20},{28,24},{5,1},{9,5},{13... | collective-permute-start | bytes 1572872 | tf_op jit(solution)/shard_map/ppermute | solution.py:21
  92.6 7.5 copy-start.1
  100.1 2.1 copy-start.4
  102.3 25.1 %collective-permute-start.4 = (bf16[1024,256]{1,0:T(8,128)(2,1)S(1)}, bf16[1024,256]{1,0:T(8,128)(2,1)S(1)}, u32[]{:S(2)}, u32[]{:S(2)}) collective-permute-start(bf16[1024,256]{1,0:T(8,128)(2,1)S(1)} %get-tuple-element.25), channel_id=1, source_target_pairs={{0,4},{4,8},{8,12},{12,16},{16,20},{20,24},{24,28},{1,5},{5,9},{9,... | collective-permute-start | bytes 1572872 | tf_op jit(solution)/shard_map/ppermute | solution.py:20
  106.7 20.7 %collective-permute-start.5 = (bf16[1024,256]{1,0:T(8,128)(2,1)S(1)}, bf16[1024,256]{1,0:T(8,128)(2,1)S(1)}, u32[]{:S(2)}, u32[]{:S(2)}) collective-permute-start(bf16[1024,256]{1,0:T(8,128)(2,1)S(1)} %get-tuple-element.26), channel_id=1, source_target_pairs={{4,0},{8,4},{12,8},{16,12},{20,16},{24,20},{28,24},{5,1},{9,5},{13... | collective-permute-start | bytes 1572872 | tf_op jit(solution)/shard_map/ppermute | solution.py:21
  138.6 7.5 copy-start.2
  138.6 8.0 %copy-start.5 = (f32[32,256,128,1]{1,2,3,0:T(8,128)S(1)}, f32[32,256,128,1]{1,2,3,0:T(8,128)}, u32[]{:S(2)}) copy-start(f32[32,256,128,1]{1,2,3,0:T(8,128)} %copy-done.4) | copy-start | bytes 12582916
  146.6 2.6 copy-start.8
  149.3 13.0 %collective-permute-start.6 = (bf16[1024,256]{1,0:T(8,128)(2,1)S(1)}, bf16[1024,256]{1,0:T(8,128)(2,1)S(1)}, u32[]{:S(2)}, u32[]{:S(2)}) collective-permute-start(bf16[1024,256]{1,0:T(8,128)(2,1)S(1)} %get-tuple-element.23), channel_id=1, source_target_pairs={{0,4},{4,8},{8,12},{12,16},{16,20},{20,24},{24,28},{1,5},{5,9},{9,... | collective-permute-start | bytes 1572872 | tf_op jit(solution)/shard_map/ppermute | solution.py:20
  153.8 20.2 %collective-permute-start.7 = (bf16[1024,256]{1,0:T(8,128)(2,1)S(1)}, bf16[1024,256]{1,0:T(8,128)(2,1)S(1)}, u32[]{:S(2)}, u32[]{:S(2)}) collective-permute-start(bf16[1024,256]{1,0:T(8,128)(2,1)S(1)} %get-tuple-element.24), channel_id=1, source_target_pairs={{4,0},{8,4},{12,8},{16,12},{20,16},{24,20},{28,24},{5,1},{9,5},{13... | collective-permute-start | bytes 1572872 | tf_op jit(solution)/shard_map/ppermute | solution.py:21
  185.3 7.5 %copy-start.3 = (f32[32,256,128,1]{1,2,3,0:T(8,128)S(1)}, f32[32,256,128,1]{1,2,3,0:T(8,128)}, u32[]{:S(2)}) copy-start(f32[32,256,128,1]{1,2,3,0:T(8,128)} %copy-done) | copy-start | bytes 12582916
  185.3 8.0 %copy-start.6 = (f32[32,256,128,1]{1,2,3,0:T(8,128)S(1)}, f32[32,256,128,1]{1,2,3,0:T(8,128)}, u32[]{:S(2)}) copy-start(f32[32,256,128,1]{1,2,3,0:T(8,128)} %copy-done.4) | copy-start | bytes 12582916
  185.3 9.2 %copy-start.9 = (f32[32,256,128,1]{1,2,3,0:T(8,128)S(1)}, f32[32,256,128,1]{1,2,3,0:T(8,128)}, u32[]{:S(2)}) copy-start(f32[32,256,128,1]{1,2,3,0:T(8,128)} %copy-done.8) | copy-start | bytes 12582916
  198.9 155.8 %all-reduce.3.cloned.1.call-start = ((), (), s32[]{:S(2)}) async-start(), calls=%async_computation.1 | async-start | bytes 2097152 | tf_op jit(solution)/shard_map/psum | solution.py:68
  276.4 114.0 %all-gather.5.cloned.1.call-start = ((), (), s32[]{:S(2)}) async-start(), calls=%async_computation.2 | async-start | bytes 5242880 | tf_op jit(solution)/shard_map/all_gather | solution.py:69
  405.4 1.9 copy-start.11
  718.2 3.2 copy-start.10
  729.5 11.2 %slice-start = ((s8[8388608]{0:T(1024)(128)(4,1)}), s8[4194304]{0:T(1024)(128)(4,1)S(1)}, s32[]{:S(2)}) async-start(s8[8388608]{0:T(1024)(128)(4,1)} %bitcast.197), calls=%async_computation.3 | async-start | bytes 8388608
  733.0 7.7 %slice-start.1 = ((s8[8388608]{0:T(1024)(128)(4,1)}), s8[4194304]{0:T(1024)(128)(4,1)S(1)}, s32[]{:S(2)}) async-start(s8[8388608]{0:T(1024)(128)(4,1)} %bitcast.197), calls=%async_computation.4 | async-start | bytes 8388608
Sparse Core Ops, SparseCore 0:
  199.0 68.8 all-gather.2
  276.5 78.1 all-reduce.2
  356.3 34.0 all-gather.4
where the time goes:
time: 763 us; the launch traced here: 755 us
  other arithmetic  287 us (38%)
  waiting for transfers between devices  258 us (34%)
  matrix products  91 us (12%)
  local copies, waits for them, and re-layouts  75.8 us (10%)
  starting transfers between devices  23.9 us (3%)
  between operations  18.8 us (2%)
    another operation x30, other arithmetic, shards(): lower = jnp.linalg.cholesky(gram_matrix)  172 us
    another operation x3, other arithmetic, shards(): lax.linalg.triangular_solve(lower, identity, left_side=True, lower=True)  83.9 us
    psum x1, waiting for transfers between devices, shards(): summed = lax.psum(panel, 'rows')  78.3 us
    all_gather x1, waiting for transfers between devices, shards(): whole_block = lax.all_gather(final, 'vecs', axis=1, tiled=True)  68.9 us
    ppermute x4, waiting for transfers between devices, with_halo(): before = lax.ppermute(last, axis, up)  66.5 us
    gather x4, local copies, waits for them, and re-layouts, product(): picked = stacked[local_index]  36.1 us
    all_gather x1, waiting for transfers between devices, shards(): lax.all_gather(summed, 'vecs', axis=0, tiled=True) / total_rows  32.8 us
    dot_general x4, matrix products, product(): jnp.einsum('rjab,rjbk->rak', blocks, picked, preferred_element_type=jnp.f...  30.1 us
  transfers between devices with their start and end apart: 11, of which 8 were waited for; matrix products, arithmetic and copies ran while one was open for 0% of the time, Pallas kernels for 0%

commit v1 on v0

v1 whole, which is shorter than its diff:
```python
import functools

import jax
import jax.numpy as jnp
from jax import lax
from jax.experimental import pallas as pl
from jax.experimental.pallas import tpu as pltpu
from jax.sharding import PartitionSpec as P

DEGREE = 4

filter_center = 0.25
filter_radius = 1.25

HIGHEST = lax.Precision.HIGHEST
VMEM_LIMIT = 56 * 1024 * 1024


def step_kernel(group, n_pieces, kind, emit_f32, index_ref, *refs):
    pieces = refs[:n_pieces]
    blocks_ref = refs[n_pieces]
    rest = refs[n_pieces + 1 :]
    if kind == "first":
        (cur_ref, *outs), old_ref = rest, None
    else:
        cur_ref, old_ref, *outs = rest
    *outs, window = outs
    step = pl.program_id(0)
    size_b = blocks_ref.shape[2]
    nnz = blocks_ref.shape[1]

    @pl.when(step == 0)
    def _():
        start = 0
        for piece in pieces:
            count = piece.shape[0]
            window[start : start + count, :] = piece[...]
            start += count

    for g in range(group):
        acc = None
        for j in range(nnz):
            at = pl.multiple_of(index_ref[(step * group + g) * nnz + j] * size_b, size_b)
            part = jnp.dot(
                blocks_ref[g, j], window[pl.ds(at, size_b), :], preferred_element_type=jnp.float32
            )
            acc = part if acc is None else acc + part
        rows = slice(g * size_b, (g + 1) * size_b)
        cur = cur_ref[rows, :].astype(jnp.float32)
        new = (acc - filter_center * cur) * (1.0 / filter_radius)
        if kind != "first":
            new = 2.0 * new - old_ref[rows, :].astype(jnp.float32)
        outs[0][rows, :] = new.astype(jnp.bfloat16)
        if emit_f32:
            outs[1][rows, :] = new


def chebyshev_step(index, pieces, blocks, row_of, count, cur, old, kind, emit_f32):
    size_b, nnz = blocks.shape[2], blocks.shape[1]
    width = pieces[0].shape[1]
    group = 4 if count % 4 == 0 else 1
    whole = lambda i, ix: (0, 0)
    part = lambda i, ix: (i, 0)
    tall = (group * size_b, width)
    in_specs = [pl.BlockSpec(p.shape, whole) for p in pieces]
    in_specs.append(
        pl.BlockSpec((group, nnz, size_b, size_b), lambda i, ix: (row_of(i, group), 0, 0, 0))
    )
    operands = list(pieces) + [blocks, cur]
    in_specs.append(pl.BlockSpec(tall, part))
    if kind != "first":
        operands.append(old)
        in_specs.append(pl.BlockSpec(tall, part))
    rows = count * size_b
    out_shape = [jax.ShapeDtypeStruct((rows, width), jnp.bfloat16)]
    if emit_f32:
        out_shape.append(jax.ShapeDtypeStruct((rows, width), jnp.float32))
    window_rows = sum(p.shape[0] for p in pieces)
    return pl.pallas_call(
        functools.partial(step_kernel, group, len(pieces), kind, emit_f32),
        grid_spec=pltpu.PrefetchScalarGridSpec(
            num_scalar_prefetch=1,
            grid=(count // group,),
            in_specs=in_specs,
            out_specs=[pl.BlockSpec(tall, part) for _ in out_shape],
            scratch_shapes=[pltpu.VMEM((window_rows, width), jnp.bfloat16)],
        ),
        out_shape=out_shape,
        compiler_params=pltpu.CompilerParams(vmem_limit_bytes=VMEM_LIMIT),
        cost_estimate=pl.CostEstimate(
            flops=2 * rows * nnz * size_b * width,
            bytes_accessed=rows * nnz * size_b * 2 + rows * width * 16,
            transcendentals=0,
        ),
    )(index, *operands)


def factor_block(block):
    size = block.shape[0]
    tiles = [block[8 * t : 8 * (t + 1), :] for t in range(size // 8)]
    lane = lax.broadcasted_iota(jnp.int32, (8, size), 1)
    sub = lax.broadcasted_iota(jnp.int32, (8, size), 0)
    for j in range(size):
        first, r = divmod(j, 8)
        at_j = lane == j
        row = jnp.broadcast_to(tiles[first][r : r + 1, :], (8, size))
        pivot = jnp.broadcast_to(row[:, j : j + 1], (8, size))
        scale = lax.rsqrt(pivot)
        scale = scale * (1.5 - 0.5 * (pivot * scale) * scale)
        scaled = jnp.where(at_j, 1.0, row) * scale
        twice = scaled * scale
        for t in range(first, size // 8):
            tile = tiles[t]
            column = jnp.broadcast_to(tile[:, j : j + 1], (8, size))
            new = jnp.where(at_j, 0.0, tile) - column * twice
            if t == first:
                new = jnp.where(sub > r, new, jnp.where(sub == r, scaled, tile))
            tiles[t] = new
    return jnp.concatenate(tiles, axis=0)


def inverse_kernel(size, total_rows, gram_ref, out_ref, work, factor):
    full = gram_ref.shape[0]
    count = full // size
    work[...] = gram_ref[...] / total_rows

    @pl.loop(0, count)
    def _(k):
        at = pl.multiple_of(k * size, size)
        done = factor_block(work[pl.ds(at, size), pl.ds(at, size)])
        down = lax.broadcasted_iota(jnp.int32, (size, size), 0)
        across = lax.broadcasted_iota(jnp.int32, (size, size), 1)
        factor[...] = jnp.where(across <= down, done, 0.0)
        for c in range(count):
            own = slice(c * size, (c + 1) * size)
            below = slice((c + 1) * size, full)

            @pl.when(k == c)
            def _():
                lower_inv = factor[...]
                left = slice(0, c * size)
                if c > 0:
                    out_ref[own, left] = jnp.dot(
                        lower_inv, work[own, left], precision=HIGHEST,
                        preferred_element_type=jnp.float32,
                    )
                out_ref[own, own] = lower_inv
                if c + 1 < count:
                    out_ref[own, below] = jnp.zeros((size, full - (c + 1) * size), jnp.float32)
                    right = jnp.dot(
                        lower_inv, work[own, below], precision=HIGHEST,
                        preferred_element_type=jnp.float32,
                    )
                    down_left = (((0,), (0,)), ((), ()))
                    work[below, below] -= lax.dot_general(
                        right, right, down_left, precision=HIGHEST,
                        preferred_element_type=jnp.float32,
                    )
                    known = slice(0, (c + 1) * size)
                    change = lax.dot_general(
                        right, out_ref[own, known], down_left, precision=HIGHEST,
                        preferred_element_type=jnp.float32,
                    )
                    if c > 0:
                        work[below, left] -= change[:, : c * size]
                    work[below, own] = -change[:, c * size :]


def inverse_factor(gram, total_rows):
    full = gram.shape[0]
    size = 128
    return pl.pallas_call(
        functools.partial(inverse_kernel, size, total_rows),
        out_shape=jax.ShapeDtypeStruct((full, full), jnp.float32),
        in_specs=[pl.BlockSpec(memory_space=pltpu.VMEM)],
        out_specs=pl.BlockSpec(memory_space=pltpu.VMEM),
        scratch_shapes=[
            pltpu.VMEM((full, full), jnp.float32),
            pltpu.VMEM((size, size), jnp.float32),
        ],
        compiler_params=pltpu.CompilerParams(vmem_limit_bytes=VMEM_LIMIT),
        cost_estimate=pl.CostEstimate(
            flops=40 * full * full * full, bytes_accessed=8 * full * full, transcendentals=full
        ),
    )(gram)


def split_apply(left_bf, factor):
    factor_high = factor.astype(jnp.bfloat16)
    factor_low = (factor - factor_high.astype(jnp.float32)).astype(jnp.bfloat16)
    first = jnp.dot(left_bf, factor_high.T, preferred_element_type=jnp.float32)
    second = jnp.dot(left_bf, factor_low.T, preferred_element_type=jnp.float32)
    return first + second


def filtered_block(vectors, blocks, columns):
    block_rows, nnz, size_b = blocks.shape[:3]
    reach = block_rows // 4
    edge = reach * size_b
    first_row = lax.axis_index("rows") * block_rows
    local = columns - first_row
    edges_index = jnp.concatenate([local[:reach], local[block_rows - reach :]], axis=0) + reach
    edges_index = edges_index.reshape(-1)
    inner_index = local[reach : block_rows - reach].reshape(-1)
    inner_rows = block_rows - 2 * reach

    axis_size = lax.axis_size("rows")
    up = [(i, i + 1) for i in range(axis_size - 1)]
    down = [(j, i) for i, j in up]

    def inner_of(i, group):
        return i + reach // group

    def edges_of(i, group):
        return jnp.where(i < reach // group, i, i + inner_rows // group)

    def halves(array):
        return jnp.concatenate([array[:edge], array[-edge:]], axis=0), array[edge:-edge]

    cur_edges, cur_inner = halves(vectors)
    bf_edges, bf_inner = cur_edges, cur_inner
    old_edges = old_inner = None
    for iteration in range(DEGREE):
        kind = "first" if iteration == 0 else "next"
        emit_f32 = iteration < DEGREE - 1
        low, high = bf_edges[:edge], bf_edges[edge:]
        before = lax.ppermute(high, "rows", up)
        after = lax.ppermute(low, "rows", down)
        own = [low, bf_inner, high]
        new_inner = chebyshev_step(
            inner_index, own, blocks, inner_of, inner_rows, cur_inner, old_inner, kind, emit_f32
        )
        new_edges = chebyshev_step(
            edges_index, [before] + own + [after], blocks, edges_of, 2 * reach,
            cur_edges, old_edges, kind, emit_f32,
        )
        old_edges, old_inner = cur_edges, cur_inner
        bf_edges, bf_inner = new_edges[0], new_inner[0]
        if emit_f32:
            cur_edges, cur_inner = new_edges[1], new_inner[1]
    return jnp.concatenate([bf_edges[:edge], bf_inner, bf_edges[edge:]], axis=0)


def shards(vectors, blocks, columns):
    total_rows = vectors.shape[0] * lax.axis_size("rows")
    final = filtered_block(vectors, blocks, columns)
    panel_width = final.shape[1]
    whole_block = lax.all_gather(final, "vecs", axis=1, tiled=True)
    panel = lax.dot_general(
        final, whole_block, (((0,), (0,)), ((), ())), preferred_element_type=jnp.float32
    )
    summed = lax.psum_scatter(panel, "rows", scatter_dimension=0, tiled=True)
    gram = lax.all_gather(summed, ("vecs", "rows"), axis=0, tiled=True)
    inverse = inverse_factor(gram, total_rows)
    own_rows = lax.dynamic_slice_in_dim(
        inverse, lax.axis_index("vecs") * panel_width, panel_width, 0
    )
    return split_apply(whole_block, own_rows)


def solution(mesh):
    in_specs = (P("rows", "vecs"), P("rows", None, None, None), P("rows", None))
    out_specs = P("rows", "vecs")
    return jax.shard_map(shards, mesh=mesh, in_specs=in_specs, out_specs=out_specs, check_vma=False)
```

time: 763 us -> 546 us (0.72)
  other arithmetic: 287 us -> 2.6 us
  Pallas kernels: 0 us -> 229 us
  matrix products: 91 us -> 18.9 us
  local copies, waits for them, and re-layouts: 75.8 us -> 13.6 us
  waiting for transfers between devices: 258 us -> 241 us
    another operation x33 -> x0, other arithmetic: 256 us -> none  [the longest x30 172 us: shards(): lower = jnp.linalg.cholesky(gram_matrix)]
    pallas_call x0 -> x9, Pallas kernels: none -> 229 us  [the longest x1 170 us: inverse_factor(): pl.pallas_call(functools.partial(inverse_kernel, size, total_rows), out_s...]
    psum x1 -> x0, waiting for transfers between devices: 78.3 us -> none  [shards(): summed = lax.psum(panel, 'rows')]
    reduce_scatter x0 -> x1, waiting for transfers between devices: none -> 64.7 us  [shards(): summed = lax.psum_scatter(panel, 'rows', scatter_dimension=0, tiled=True)]
    another operation x29 -> x0, matrix products: 45.4 us -> none  [the longest x14 23 us: shards(): lower = jnp.linalg.cholesky(gram_matrix)]
    gather x4 -> x0, local copies, waits for them, and re-layouts: 36.1 us -> none  [product(): picked = stacked[local_index]]
    dot_general x5 -> x1, matrix products: 38.6 us -> 6.71 us  [shards(): lax.dot_general(final, whole_block, (((0,), (0,)), ((), ())), preferred_e...]
    all_gather x1, waiting for transfers between devices: 32.8 us -> 63.8 us  [shards(): gram = lax.all_gather(summed, ('vecs', 'rows'), axis=0, tiled=True)]
  transfers between devices with their start and end apart: 11 -> 11, of which waited for: 8 -> 10; matrix products, arithmetic and copies ran while one was open for 0% -> 1% of each run, Pallas kernels for 0% -> 5%
where the time goes in v1:
time: 546 us; the launch traced here: 545 us
  waiting for transfers between devices  241 us (44%)
  Pallas kernels  229 us (42%)
  starting transfers between devices  26 us (5%)
  matrix products  18.9 us (3%)
  local copies, waits for them, and re-layouts  13.6 us (2%)
  between operations  13.3 us (2%)
    pallas_call x1, Pallas kernels, inverse_factor(): pl.pallas_call(functools.partial(inverse_kernel, size, total_rows), out_s...  170 us
    reduce_scatter x1, waiting for transfers between devices, shards(): summed = lax.psum_scatter(panel, 'rows', scatter_dimension=0, tiled=True)  64.7 us
    all_gather x1, waiting for transfers between devices, shards(): gram = lax.all_gather(summed, ('vecs', 'rows'), axis=0, tiled=True)  63.8 us
    all_gather x1, waiting for transfers between devices, shards(): whole_block = lax.all_gather(final, 'vecs', axis=1, tiled=True)  60.7 us
    pallas_call x8, Pallas kernels, chebyshev_step(): pl.pallas_call(functools.partial(step_kernel, group, len(pieces), kind, e...  58.9 us
    ppermute x4, waiting for transfers between devices, filtered_block(): before = lax.ppermute(high, 'rows', up)  41.1 us
    ppermute x4, starting transfers between devices, filtered_block(): before = lax.ppermute(high, 'rows', up)  20.7 us
  transfers between devices with their start and end apart: 11, of which 10 were waited for; matrix products, arithmetic and copies ran while one was open for 1% of the time, Pallas kernels for 5%

profile of v1, /device:TPU:0, one launch (start us, length us, event | category | flops | bytes accessed | tf_op | source)
XLA Modules:
  0.0 544.9 jit_solution(5270344982715889780)
XLA Ops:
  6.5 1.3 fusion.4
  7.8 1.3 collective-permute-start.1
  9.1 5.6 %collective-permute-start = (bf16[1024,256]{1,0:T(8,128)(2,1)S(1)}, bf16[1024,256]{1,0:T(8,128)(2,1)S(1)}, u32[]{:S(2)}, u32[]{:S(2)}) collective-permute-start(bf16[1024,256]{1,0:T(8,128)(2,1)S(1)} %get-tuple-element.30.refs_3_.refs_2_), channel_id=1, source_target_pairs={{0,4},{4,8},{8,12},{12,16},{16,20},{20,24},{24,28},{1,5},{5,9},{9,... | collective-permute-start | bytes 1572872 | tf_op jit(solution)/shard_map/ppermute | solution.py:227
  14.7 2.3 slice.46.refs_2_.refs_1_.refs_4_.refs_5_
  17.0 0.1 fusion.9
  17.1 0.1 add_add_fusion
  17.1 0.1 copy.6
  17.2 0.7 add.20.index_ref
  17.9 1.1 pad_maximum_fusion.1.refs_6_.refs_7_
  19.0 5.7 %collective-permute-done.1.refs_4_ = bf16[1024,256]{1,0:T(8,128)(2,1)S(1)} collective-permute-done((bf16[1024,256]{1,0:T(8,128)(2,1)S(1)}, bf16[1024,256]{1,0:T(8,128)(2,1)S(1)}, u32[]{:S(2)}, u32[]{:S(2)}) %collective-permute-start.1) | collective-permute-done | bytes 524320 | tf_op jit(solution)/shard_map/ppermute | solution.py:228
  24.7 11.4 %collective-permute-done.refs_0_ = bf16[1024,256]{1,0:T(8,128)(2,1)S(1)} collective-permute-done((bf16[1024,256]{1,0:T(8,128)(2,1)S(1)}, bf16[1024,256]{1,0:T(8,128)(2,1)S(1)}, u32[]{:S(2)}, u32[]{:S(2)}) %collective-permute-start) | collective-permute-done | bytes 524320 | tf_op jit(solution)/shard_map/ppermute | solution.py:227
  36.1 0.8 copy-done.11
  36.9 7.0 %shard_map.37 = (bf16[2048,256]{1,0:T(8,128)(2,1)}, f32[2048,256]{1,0:T(8,128)}) custom-call(s32[80]{0:T(128)} %add.20.index_ref, bf16[1024,256]{1,0:T(8,128)(2,1)} %copy-done.11, bf16[1024,256]{1,0:T(8,128)(2,1)} %copy-done.1, bf16[2048,256]{1,0:T(8,128)(2,1)} %slice.46.refs_2_.refs_1_.refs_4_.refs_5_, bf16[1024,256]{1,0:T(8,128)(2,1)} %copy-done.2, ...), custom_call_target="tpu_custom_call" | custom-call | flops 671088640 | bytes 11010048 | tf_op jit(solution)/shard_map/pallas_call | solution.py:79
  43.9 1.3 fusion.8
  45.2 1.3 collective-permute-start.3
  46.5 5.0 collective-permute-start.2
  51.6 0.1 copy.7
  51.7 0.7 reshape.7.index_ref
  52.4 6.9 %shard_map.38 = (bf16[2048,256]{1,0:T(8,128)(2,1)}, f32[2048,256]{1,0:T(8,128)}) custom-call(s32[80]{0:T(128)} %reshape.7.index_ref, bf16[1024,256]{1,0:T(8,128)(2,1)} %copy-done.1, bf16[2048,256]{1,0:T(8,128)(2,1)} %slice.46.refs_2_.refs_1_.refs_4_.refs_5_, bf16[1024,256]{1,0:T(8,128)(2,1)} %copy-done.2, bf16[32,5,128,128]{3,2,1,0:T(8,128)(2,1)} %refs_3_.7, ...), custom_call_target="tpu_custom_call" | custom-call | flops 671088640 | bytes 11010048 | tf_op jit(solution)/shard_map/pallas_call | solution.py:79
  59.3 2.4 collective-permute-done.3.refs_4_
  61.6 11.4 %collective-permute-done.2.refs_0_ = bf16[1024,256]{1,0:T(8,128)(2,1)S(1)} collective-permute-done((bf16[1024,256]{1,0:T(8,128)(2,1)S(1)}, bf16[1024,256]{1,0:T(8,128)(2,1)S(1)}, u32[]{:S(2)}, u32[]{:S(2)}) %collective-permute-start.2) | collective-permute-done | bytes 524320 | tf_op jit(solution)/shard_map/ppermute | solution.py:227
  73.0 0.8 copy-done.14
  73.9 7.7 %shard_map.39 = (bf16[2048,256]{1,0:T(8,128)(2,1)}, f32[2048,256]{1,0:T(8,128)}) custom-call(s32[80]{0:T(128)} %add.20.index_ref, bf16[1024,256]{1,0:T(8,128)(2,1)} %copy-done.14, bf16[1024,256]{1,0:T(8,128)(2,1)} %copy-done.5, bf16[2048,256]{1,0:T(8,128)(2,1)} %get-tuple-element.18.refs_2_.refs_1_, bf16[1024,256]{1,0:T(8,128)(2,1)} %copy-done.6, ...), custom_call_target="tpu_custom_call" | custom-call | flops 671088640 | bytes 11010048 | tf_op jit(solution)/shard_map/pallas_call | solution.py:79
  81.6 1.3 fusion.7
  82.9 1.3 collective-permute-start.5
  84.2 5.0 collective-permute-start.4
  89.2 7.4 %shard_map.40 = (bf16[2048,256]{1,0:T(8,128)(2,1)}, f32[2048,256]{1,0:T(8,128)}) custom-call(s32[80]{0:T(128)} %reshape.7.index_ref, bf16[1024,256]{1,0:T(8,128)(2,1)} %copy-done.5, bf16[2048,256]{1,0:T(8,128)(2,1)} %get-tuple-element.18.refs_2_.refs_1_, bf16[1024,256]{1,0:T(8,128)(2,1)} %copy-done.6, bf16[32,5,128,128]{3,2,1,0:T(8,128)(2,1)} %refs_3_.7, ...), custom_call_target="tpu_custom_call" | custom-call | flops 671088640 | bytes 11010048 | tf_op jit(solution)/shard_map/pallas_call | solution.py:79
  96.6 2.8 collective-permute-done.5.refs_4_
  99.4 11.4 %collective-permute-done.4.refs_0_ = bf16[1024,256]{1,0:T(8,128)(2,1)S(1)} collective-permute-done((bf16[1024,256]{1,0:T(8,128)(2,1)S(1)}, bf16[1024,256]{1,0:T(8,128)(2,1)S(1)}, u32[]{:S(2)}, u32[]{:S(2)}) %collective-permute-start.4) | collective-permute-done | bytes 524320 | tf_op jit(solution)/shard_map/ppermute | solution.py:227
  110.8 0.8 copy-done.15
  111.6 8.0 %shard_map.41 = (bf16[2048,256]{1,0:T(8,128)(2,1)}, f32[2048,256]{1,0:T(8,128)}) custom-call(s32[80]{0:T(128)} %add.20.index_ref, bf16[1024,256]{1,0:T(8,128)(2,1)} %copy-done.15, bf16[1024,256]{1,0:T(8,128)(2,1)} %copy-done.3, bf16[2048,256]{1,0:T(8,128)(2,1)} %get-tuple-element.22.refs_2_.refs_1_, bf16[1024,256]{1,0:T(8,128)(2,1)} %copy-done.4, ...), custom_call_target="tpu_custom_call" | custom-call | flops 671088640 | bytes 11010048 | tf_op jit(solution)/shard_map/pallas_call | solution.py:79
  119.5 1.3 fusion.6
  120.8 1.3 collective-permute-start.7
  122.1 5.0 collective-permute-start.6
  127.2 7.5 %shard_map.42 = (bf16[2048,256]{1,0:T(8,128)(2,1)}, f32[2048,256]{1,0:T(8,128)}) custom-call(s32[80]{0:T(128)} %reshape.7.index_ref, bf16[1024,256]{1,0:T(8,128)(2,1)} %copy-done.3, bf16[2048,256]{1,0:T(8,128)(2,1)} %get-tuple-element.22.refs_2_.refs_1_, bf16[1024,256]{1,0:T(8,128)(2,1)} %copy-done.4, bf16[32,5,128,128]{3,2,1,0:T(8,128)(2,1)} %refs_3_.7, ...), custom_call_target="tpu_custom_call" | custom-call | flops 671088640 | bytes 11010048 | tf_op jit(solution)/shard_map/pallas_call | solution.py:79
  134.7 7.0 %shard_map.44 = bf16[2048,256]{1,0:T(8,128)(2,1)} custom-call(s32[80]{0:T(128)} %reshape.7.index_ref, bf16[1024,256]{1,0:T(8,128)(2,1)} %copy-done.7, bf16[2048,256]{1,0:T(8,128)(2,1)} %get-tuple-element.26.refs_2_.refs_1_, bf16[1024,256]{1,0:T(8,128)(2,1)} %copy-done.8, bf16[32,5,128,128]{3,2,1,0:T(8,128)(2,1)} %refs_3_.7, ...), custom_call_target="tpu_custom_call" | custom-call | flops 671088640 | bytes 11010048 | tf_op jit(solution)/shard_map/pallas_call | solution.py:79
  141.7 7.0 %collective-permute-done.6.refs_0_ = bf16[1024,256]{1,0:T(8,128)(2,1)S(1)} collective-permute-done((bf16[1024,256]{1,0:T(8,128)(2,1)S(1)}, bf16[1024,256]{1,0:T(8,128)(2,1)S(1)}, u32[]{:S(2)}, u32[]{:S(2)}) %collective-permute-start.6) | collective-permute-done | bytes 524320 | tf_op jit(solution)/shard_map/ppermute | solution.py:227
  148.7 0.8 copy-done.17
  149.5 7.5 %shard_map.43 = bf16[2048,256]{1,0:T(8,128)(2,1)} custom-call(s32[80]{0:T(128)} %add.20.index_ref, bf16[1024,256]{1,0:T(8,128)(2,1)} %copy-done.17, bf16[1024,256]{1,0:T(8,128)(2,1)} %copy-done.7, bf16[2048,256]{1,0:T(8,128)(2,1)} %get-tuple-element.26.refs_2_.refs_1_, bf16[1024,256]{1,0:T(8,128)(2,1)} %copy-done.8, bf16[1024,256]{1,0:T(8,128)(2,1)} %copy-done.16, ...), custom_call_target="tpu_custom_call" | custom-call | flops 671088640 | bytes 11010048 | tf_op jit(solution)/shard_map/pallas_call | solution.py:79
  157.0 1.3 fusion.5
  158.3 1.5 pad_maximum_fusion
  159.8 60.7 %all-gather.3.cloned.1.call-done = bf16[4096,1024]{1,0:T(8,128)(2,1)} async-done(((bf16[4096,256]{1,0:T(8,128)(2,1)}), bf16[4096,1024]{1,0:T(8,128)(2,1)}) %all-gather.3.cloned.1.call-update) | async-done | bytes 8388624 | tf_op jit(solution)/shard_map/all_gather | solution.py:248
  220.5 6.7 %fusion.3 = f32[256,1024]{1,0:T(8,128)} fusion(bf16[4096,1024]{1,0:T(8,128)(2,1)} %all-gather.3.cloned.1.call-done, bf16[1024,256]{1,0:T(8,128)(2,1)S(1)} %get-tuple-element.32, bf16[2048,256]{1,0:T(8,128)(2,1)S(1)} %copy-done.9, bf16[1024,256]{1,0:T(8,128)(2,1)S(1)} %get-tuple-element.31), kind=kOutput, calls=%fused_computation.10 | convolution fusion | flops 2153775104 | bytes 11534336 | tf_op jit(solution)/shard_map/dot_general | solution.py:249
  227.2 64.7 %reduce-scatter.2.cloned.1.call-done = f32[32,1024]{1,0:T(8,128)} async-done(((f32[256,1024]{1,0:T(8,128)}), f32[32,1024]{1,0:T(8,128)}) %reduce-scatter.2.cloned.1.call-update) | async-done | bytes 131088 | tf_op jit(solution)/shard_map/reduce_scatter | solution.py:252
  292.0 63.8 %all-gather.5.cloned.1.call-done.gram_ref = f32[1024,1024]{1,0:T(8,128)} async-done(((f32[32,1024]{1,0:T(8,128)}), f32[1024,1024]{1,0:T(8,128)}) %all-gather.5.cloned.1.call-update) | async-done | bytes 4194320 | tf_op jit(solution)/shard_map/all_gather | solution.py:253
  355.8 170.5 %shard_map.45 = f32[1024,1024]{1,0:T(8,128)} custom-call(f32[1024,1024]{1,0:T(8,128)} %all-gather.5.cloned.1.call-done.gram_ref), custom_call_target="tpu_custom_call" | custom-call | flops 42949672960 | bytes 8388608 | tf_op jit(solution)/shard_map/pallas_call | solution.py:172
  526.2 6.2 %fusion = f32[4096,256]{1,0:T(8,128)S(1)} fusion(bf16[4096,1024]{1,0:T(8,128)(2,1)} %all-gather.3.cloned.1.call-done, f32[1024,1024]{1,0:T(8,128)} %shard_map.45, s32[]{:T(128)S(6)} %select_n.3), kind=kOutput, calls=%fused_computation.5 | convolution fusion | flops 2147483648 | bytes 13107204 | tf_op jit(solution)/shard_map/dot_general | solution.py:191
  532.5 5.9 %convolution_add_fusion = f32[4096,256]{1,0:T(8,128)} fusion(f32[4096,256]{1,0:T(8,128)S(1)} %fusion, bf16[4096,1024]{1,0:T(8,128)(2,1)S(1)} %copy-done, f32[1024,1024]{1,0:T(8,128)} %shard_map.45, s32[]{:T(128)S(6)} %select_n.3), kind=kOutput, calls=%fused_computation | convolution fusion | flops 2149580800 | bytes 17825796 | tf_op jit(solution)/shard_map/dot_general | solution.py:192
  (43 shorter events, 0.3 us)
Async XLA Ops:
  6.5 10.5 %copy-start.18 = (s32[32,5]{0,1:T(8,128)S(1)}, s32[32,5]{0,1:T(8,128)}, u32[]{:S(2)}) copy-start(s32[32,5]{0,1:T(8,128)} %param.5) | copy-start | bytes 1924
  6.5 213.9 %all-gather.3.cloned.1.call-start = ((), (), s32[]{:S(2)}) async-start(), calls=%async_computation.1 | async-start | bytes 10485760 | tf_op jit(solution)/shard_map/all_gather | solution.py:248
  7.8 28.2 %copy-start.1 = (bf16[1024,256]{1,0:T(8,128)(2,1)}, bf16[1024,256]{1,0:T(8,128)(2,1)S(1)}, u32[]{:S(2)}) copy-start(bf16[1024,256]{1,0:T(8,128)(2,1)S(1)} %get-tuple-element.29.refs_1_.refs_0_) | copy-start | bytes 1572868
  7.8 28.2 %copy-start.2 = (bf16[1024,256]{1,0:T(8,128)(2,1)}, bf16[1024,256]{1,0:T(8,128)(2,1)S(1)}, u32[]{:S(2)}) copy-start(bf16[1024,256]{1,0:T(8,128)(2,1)S(1)} %get-tuple-element.30.refs_3_.refs_2_) | copy-start | bytes 1572868
  7.8 16.8 %collective-permute-start.1 = (bf16[1024,256]{1,0:T(8,128)(2,1)S(1)}, bf16[1024,256]{1,0:T(8,128)(2,1)S(1)}, u32[]{:S(2)}, u32[]{:S(2)}) collective-permute-start(bf16[1024,256]{1,0:T(8,128)(2,1)S(1)} %get-tuple-element.29.refs_1_.refs_0_), channel_id=1, source_target_pairs={{4,0},{8,4},{12,8},{16,12},{20,16},{24,20},{28,24},{5,1},{9,5},{13... | collective-permute-start | bytes 1572872 | tf_op jit(solution)/shard_map/ppermute | solution.py:228
  9.1 26.9 %collective-permute-start = (bf16[1024,256]{1,0:T(8,128)(2,1)S(1)}, bf16[1024,256]{1,0:T(8,128)(2,1)S(1)}, u32[]{:S(2)}, u32[]{:S(2)}) collective-permute-start(bf16[1024,256]{1,0:T(8,128)(2,1)S(1)} %get-tuple-element.30.refs_3_.refs_2_), channel_id=1, source_target_pairs={{0,4},{4,8},{8,12},{12,16},{16,20},{20,24},{24,28},{1,5},{5,9},{9,... | collective-permute-start | bytes 1572872 | tf_op jit(solution)/shard_map/ppermute | solution.py:227
  24.7 11.4 %copy-start.10 = (bf16[1024,256]{1,0:T(8,128)(2,1)}, bf16[1024,256]{1,0:T(8,128)(2,1)S(1)}, u32[]{:S(2)}) copy-start(bf16[1024,256]{1,0:T(8,128)(2,1)S(1)} %collective-permute-done.1.refs_4_) | copy-start | bytes 1572868
  36.1 0.8 copy-start.11
  45.1 14.1 %copy-start.5 = (bf16[1024,256]{1,0:T(8,128)(2,1)}, bf16[1024,256]{1,0:T(8,128)(2,1)S(1)}, u32[]{:S(2)}) copy-start(bf16[1024,256]{1,0:T(8,128)(2,1)S(1)} %get-tuple-element.37.refs_1_.refs_0_) | copy-start | bytes 1572868
  45.1 14.1 %copy-start.6 = (bf16[1024,256]{1,0:T(8,128)(2,1)}, bf16[1024,256]{1,0:T(8,128)(2,1)S(1)}, u32[]{:S(2)}) copy-start(bf16[1024,256]{1,0:T(8,128)(2,1)S(1)} %get-tuple-element.38.refs_3_.refs_2_) | copy-start | bytes 1572868
  45.2 16.5 %collective-permute-start.3 = (bf16[1024,256]{1,0:T(8,128)(2,1)S(1)}, bf16[1024,256]{1,0:T(8,128)(2,1)S(1)}, u32[]{:S(2)}, u32[]{:S(2)}) collective-permute-start(bf16[1024,256]{1,0:T(8,128)(2,1)S(1)} %get-tuple-element.37.refs_1_.refs_0_), channel_id=1, source_target_pairs={{4,0},{8,4},{12,8},{16,12},{20,16},{24,20},{28,24},{5,1},{9,5},{13... | collective-permute-start | bytes 1572872 | tf_op jit(solution)/shard_map/ppermute | solution.py:228
  46.5 26.6 %collective-permute-start.2 = (bf16[1024,256]{1,0:T(8,128)(2,1)S(1)}, bf16[1024,256]{1,0:T(8,128)(2,1)S(1)}, u32[]{:S(2)}, u32[]{:S(2)}) collective-permute-start(bf16[1024,256]{1,0:T(8,128)(2,1)S(1)} %get-tuple-element.38.refs_3_.refs_2_), channel_id=1, source_target_pairs={{0,4},{4,8},{8,12},{12,16},{16,20},{20,24},{24,28},{1,5},{5,9},{9,... | collective-permute-start | bytes 1572872 | tf_op jit(solution)/shard_map/ppermute | solution.py:227
  61.6 11.4 %copy-start.12 = (bf16[1024,256]{1,0:T(8,128)(2,1)}, bf16[1024,256]{1,0:T(8,128)(2,1)S(1)}, u32[]{:S(2)}) copy-start(bf16[1024,256]{1,0:T(8,128)(2,1)S(1)} %collective-permute-done.3.refs_4_) | copy-start | bytes 1572868
  73.0 0.8 copy-start.14
  82.9 13.7 %copy-start.3 = (bf16[1024,256]{1,0:T(8,128)(2,1)}, bf16[1024,256]{1,0:T(8,128)(2,1)S(1)}, u32[]{:S(2)}) copy-start(bf16[1024,256]{1,0:T(8,128)(2,1)S(1)} %get-tuple-element.35.refs_1_.refs_0_) | copy-start | bytes 1572868
  82.9 13.7 %copy-start.4 = (bf16[1024,256]{1,0:T(8,128)(2,1)}, bf16[1024,256]{1,0:T(8,128)(2,1)S(1)}, u32[]{:S(2)}) copy-start(bf16[1024,256]{1,0:T(8,128)(2,1)S(1)} %get-tuple-element.36.refs_3_.refs_2_) | copy-start | bytes 1572868
  82.9 16.5 %collective-permute-start.5 = (bf16[1024,256]{1,0:T(8,128)(2,1)S(1)}, bf16[1024,256]{1,0:T(8,128)(2,1)S(1)}, u32[]{:S(2)}, u32[]{:S(2)}) collective-permute-start(bf16[1024,256]{1,0:T(8,128)(2,1)S(1)} %get-tuple-element.35.refs_1_.refs_0_), channel_id=1, source_target_pairs={{4,0},{8,4},{12,8},{16,12},{20,16},{24,20},{28,24},{5,1},{9,5},{13... | collective-permute-start | bytes 1572872 | tf_op jit(solution)/shard_map/ppermute | solution.py:228
  84.2 26.6 %collective-permute-start.4 = (bf16[1024,256]{1,0:T(8,128)(2,1)S(1)}, bf16[1024,256]{1,0:T(8,128)(2,1)S(1)}, u32[]{:S(2)}, u32[]{:S(2)}) collective-permute-start(bf16[1024,256]{1,0:T(8,128)(2,1)S(1)} %get-tuple-element.36.refs_3_.refs_2_), channel_id=1, source_target_pairs={{0,4},{4,8},{8,12},{12,16},{16,20},{20,24},{24,28},{1,5},{5,9},{9,... | collective-permute-start | bytes 1572872 | tf_op jit(solution)/shard_map/ppermute | solution.py:227
  99.4 11.4 %copy-start.13 = (bf16[1024,256]{1,0:T(8,128)(2,1)}, bf16[1024,256]{1,0:T(8,128)(2,1)S(1)}, u32[]{:S(2)}) copy-start(bf16[1024,256]{1,0:T(8,128)(2,1)S(1)} %collective-permute-done.5.refs_4_) | copy-start | bytes 1572868
  110.8 0.8 copy-start.15
  120.8 13.9 %copy-start.7 = (bf16[1024,256]{1,0:T(8,128)(2,1)}, bf16[1024,256]{1,0:T(8,128)(2,1)S(1)}, u32[]{:S(2)}) copy-start(bf16[1024,256]{1,0:T(8,128)(2,1)S(1)} %get-tuple-element.33.refs_1_.refs_0_) | copy-start | bytes 1572868
  120.8 13.9 %copy-start.8 = (bf16[1024,256]{1,0:T(8,128)(2,1)}, bf16[1024,256]{1,0:T(8,128)(2,1)S(1)}, u32[]{:S(2)}) copy-start(bf16[1024,256]{1,0:T(8,128)(2,1)S(1)} %get-tuple-element.34.refs_3_.refs_2_) | copy-start | bytes 1572868
  120.8 20.9 %collective-permute-start.7 = (bf16[1024,256]{1,0:T(8,128)(2,1)S(1)}, bf16[1024,256]{1,0:T(8,128)(2,1)S(1)}, u32[]{:S(2)}, u32[]{:S(2)}) collective-permute-start(bf16[1024,256]{1,0:T(8,128)(2,1)S(1)} %get-tuple-element.33.refs_1_.refs_0_), channel_id=1, source_target_pairs={{4,0},{8,4},{12,8},{16,12},{20,16},{24,20},{28,24},{5,1},{9,5},{13... | collective-permute-start | bytes 1572872 | tf_op jit(solution)/shard_map/ppermute | solution.py:228
  122.1 26.6 %collective-permute-start.6 = (bf16[1024,256]{1,0:T(8,128)(2,1)S(1)}, bf16[1024,256]{1,0:T(8,128)(2,1)S(1)}, u32[]{:S(2)}, u32[]{:S(2)}) collective-permute-start(bf16[1024,256]{1,0:T(8,128)(2,1)S(1)} %get-tuple-element.34.refs_3_.refs_2_), channel_id=1, source_target_pairs={{0,4},{4,8},{8,12},{12,16},{16,20},{20,24},{24,28},{1,5},{5,9},{9,... | collective-permute-start | bytes 1572872 | tf_op jit(solution)/shard_map/ppermute | solution.py:227
  141.7 7.0 %copy-start.16 = (bf16[1024,256]{1,0:T(8,128)(2,1)}, bf16[1024,256]{1,0:T(8,128)(2,1)S(1)}, u32[]{:S(2)}) copy-start(bf16[1024,256]{1,0:T(8,128)(2,1)S(1)} %collective-permute-done.7.refs_4_) | copy-start | bytes 1572868
  148.7 0.8 copy-start.17
  149.5 8.8 %copy-start.9 = (bf16[2048,256]{1,0:T(8,128)(2,1)S(1)}, bf16[2048,256]{1,0:T(8,128)(2,1)}, u32[]{:S(2)}) copy-start(bf16[2048,256]{1,0:T(8,128)(2,1)} %shard_map.44) | copy-start | bytes 3145732
  159.7 132.2 %reduce-scatter.2.cloned.1.call-start = ((), (), s32[]{:S(2)}) async-start(), calls=%async_computation.2 | async-start | bytes 1179648 | tf_op jit(solution)/shard_map/reduce_scatter | solution.py:252
  227.2 128.6 %all-gather.5.cloned.1.call-start = ((), (), s32[]{:S(2)}) async-start(), calls=%async_computation.3 | async-start | bytes 4325376 | tf_op jit(solution)/shard_map/all_gather | solution.py:253
  526.2 6.2 %copy-start = (bf16[4096,1024]{1,0:T(8,128)(2,1)S(1)}, bf16[4096,1024]{1,0:T(8,128)(2,1)}, u32[]{:S(2)}) copy-start(bf16[4096,1024]{1,0:T(8,128)(2,1)} %all-gather.3.cloned.1.call-done) | copy-start | bytes 25165828
Sparse Core Ops, SparseCore 0:
  159.9 60.5 all-gather.2
  227.3 64.5 reduce-scatter.1
  295.0 60.7 all-gather.4

commit v2 on v1

--- a/solution.py
+++ b/solution.py
@@ -14,6 +14,7 @@
 
 HIGHEST = lax.Precision.HIGHEST
 VMEM_LIMIT = 56 * 1024 * 1024
+PIVOTS = 8
 
 
 def step_kernel(group, n_pieces, kind, emit_f32, index_ref, *refs):
@@ -100,29 +101,71 @@
     tiles = [block[8 * t : 8 * (t + 1), :] for t in range(size // 8)]
     lane = lax.broadcasted_iota(jnp.int32, (8, size), 1)
     sub = lax.broadcasted_iota(jnp.int32, (8, size), 0)
-    for j in range(size):
+
+    def spread(array):
+        return jnp.broadcast_to(array, (8, size))
+
+    for j in range(0, size, PIVOTS):
         first, r = divmod(j, 8)
-        at_j = lane == j
-        row = jnp.broadcast_to(tiles[first][r : r + 1, :], (8, size))
-        pivot = jnp.broadcast_to(row[:, j : j + 1], (8, size))
-        scale = lax.rsqrt(pivot)
-        scale = scale * (1.5 - 0.5 * (pivot * scale) * scale)
-        scaled = jnp.where(at_j, 1.0, row) * scale
-        twice = scaled * scale
-        for t in range(first, size // 8):
+        each = range(PIVOTS)
+        at_any = jnp.logical_and(lane >= j, lane < j + PIVOTS)
+        head = tiles[first]
+        cols = [spread(head[:, j + a : j + a + 1]) for a in each]
+        pivots = [[spread(cols[a][r + b : r + b + 1, :]) for a in range(b + 1)] for b in each]
+        rows = [jnp.where(at_any, 0.0, spread(head[r + a : r + a + 1, :])) for a in each]
+        rows = [jnp.where(lane == j + a, 1.0, rows[a]) for a in each]
+        over, ratio = [], {}
+        for a in each:
+            over.append(1.0 / pivots[a][a])
+            for b in range(a + 1, PIVOTS):
+                ratio[b, a] = pivots[b][a] * over[a]
+                for c in range(a + 1, b + 1):
+                    pivots[b][c] = pivots[b][c] - ratio[b, a] * pivots[c][a]
+                rows[b] = rows[b] - ratio[b, a] * rows[a]
+        use = [None] * PIVOTS
+        for a in reversed(each):
+            use[a] = rows[a] * over[a]
+            for b in range(a + 1, PIVOTS):
+                use[a] = use[a] - ratio[b, a] * use[b]
+        start = first if r + PIVOTS < 8 else first + 1
+        for t in range(start, size // 8):
             tile = tiles[t]
-            column = jnp.broadcast_to(tile[:, j : j + 1], (8, size))
-            new = jnp.where(at_j, 0.0, tile) - column * twice
-            if t == first:
-                new = jnp.where(sub > r, new, jnp.where(sub == r, scaled, tile))
-            tiles[t] = new
+            if t > first:
+                cols = [spread(tile[:, j + a : j + a + 1]) for a in each]
+            terms = [cols[a] * use[a] for a in each]
+            while len(terms) > 1:
+                terms = [x + y for x, y in zip(terms[::2], terms[1::2])]
+            tiles[t] = jnp.where(at_any, 0.0, tile) - terms[0]
+        top = jnp.where(sub < r, head, tiles[first])
+        for a in each:
+            top = jnp.where(sub == r + a, rows[a] * lax.rsqrt(pivots[a][a]), top)
+        tiles[first] = top
     return jnp.concatenate(tiles, axis=0)
 
 
-def inverse_kernel(size, total_rows, gram_ref, out_ref, work, factor):
+def inverse_kernel(size, total_rows, panels, gram_ref, out_ref, work, factor):
     full = gram_ref.shape[0]
     count = full // size
-    work[...] = gram_ref[...] / total_rows
+    wide = full // panels
+    half = panels // 2
+    work[...] = jnp.zeros_like(work)
+    for low in range(panels):
+        for high in range(low, panels):
+            apart = high - low
+            own, other = slice(low * wide, (low + 1) * wide), slice(high * wide, (high + 1) * wide)
+            if not shared(panels, wide):
+                work[own, other] = gram_ref[own, other] / total_rows
+            elif apart < half:
+                work[own, other] = gram_ref[own, apart * wide : (apart + 1) * wide] / total_rows
+            elif apart > half:
+                back = panels - apart
+                part = gram_ref[other, back * wide : (back + 1) * wide] / total_rows
+                work[own, other] = part.T
+            else:
+                middle = high * wide + wide // 2
+                last = slice(half * wide, half * wide + wide // 2)
+                work[own, high * wide : middle] = gram_ref[own, last] / total_rows
+                work[own, middle : (high + 1) * wide] = gram_ref[other, last] / total_rows
 
     @pl.loop(0, count)
     def _(k):
@@ -166,11 +209,27 @@
                     work[below, own] = -change[:, c * size :]
 
 
-def inverse_factor(gram, total_rows):
+def shared(panels, wide):
+    return panels % 2 == 0 and wide % 256 == 0
+
+
+def panel_part(panel):
+    panels, wide = lax.axis_size("vecs"), panel.shape[0]
+    if not shared(panels, wide):
+        return panel
+    me, half, short = lax.axis_index("vecs"), panels // 2, wide // 2
+    twice = jnp.concatenate([panel, panel], axis=1)
+    near = lax.dynamic_slice_in_dim(twice, me * wide, half * wide, 1)
+    far = lax.dynamic_slice_in_dim(twice, (me + half) * wide, wide, 1)
+    middle = jnp.where(me < half, far[:, :short], far[short:, :].T)
+    return jnp.concatenate([near, middle], axis=1)
+
+
+def inverse_factor(gram, total_rows, panels):
     full = gram.shape[0]
     size = 128
     return pl.pallas_call(
-        functools.partial(inverse_kernel, size, total_rows),
+        functools.partial(inverse_kernel, size, total_rows, panels),
         out_shape=jax.ShapeDtypeStruct((full, full), jnp.float32),
         in_specs=[pl.BlockSpec(memory_space=pltpu.VMEM)],
         out_specs=pl.BlockSpec(memory_space=pltpu.VMEM),
@@ -249,9 +308,9 @@
     panel = lax.dot_general(
         final, whole_block, (((0,), (0,)), ((), ())), preferred_element_type=jnp.float32
     )
-    summed = lax.psum_scatter(panel, "rows", scatter_dimension=0, tiled=True)
-    gram = lax.all_gather(summed, ("vecs", "rows"), axis=0, tiled=True)
-    inverse = inverse_factor(gram, total_rows)
+    summed = lax.psum(panel_part(panel), "rows")
+    gram = lax.all_gather(summed, "vecs", axis=0, tiled=True)
+    inverse = inverse_factor(gram, total_rows, lax.axis_size("vecs"))
     own_rows = lax.dynamic_slice_in_dim(
         inverse, lax.axis_index("vecs") * panel_width, panel_width, 0
     )

time: 546 us -> 417 us (0.76)
  Pallas kernels: 229 us -> 125 us
  waiting for transfers between devices: 241 us -> 213 us
    pallas_call x1, Pallas kernels: 170 us -> 65.6 us  [inverse_factor(): pl.pallas_call(functools.partial(inverse_kernel, size, total_rows, panels...]
    psum x0 -> x1, waiting for transfers between devices: none -> 73.8 us  [shards(): summed = lax.psum(panel_part(panel), 'rows')]
    reduce_scatter x1 -> x0, waiting for transfers between devices: 64.7 us -> none  [shards(): summed = lax.psum_scatter(panel, 'rows', scatter_dimension=0, tiled=True)]
    all_gather x1, waiting for transfers between devices: 63.8 us -> 26.5 us  [shards(): gram = lax.all_gather(summed, 'vecs', axis=0, tiled=True)]
  transfers between devices with their start and end apart: 11 -> 11, of which waited for: 10 -> 10; matrix products, arithmetic and copies ran while one was open for 1% -> 1% of each run, Pallas kernels for 5% -> 7%
where the time goes in v2:
time: 417 us; the launch traced here: 416 us
  waiting for transfers between devices  213 us (51%)
  Pallas kernels  125 us (30%)
  starting transfers between devices  26 us (6%)
  matrix products  21.2 us (5%)
  local copies, waits for them, and re-layouts  13.8 us (3%)
  between operations  13.4 us (3%)
    psum x1, waiting for transfers between devices, shards(): summed = lax.psum(panel_part(panel), 'rows')  73.8 us
    pallas_call x1, Pallas kernels, inverse_factor(): pl.pallas_call(functools.partial(inverse_kernel, size, total_rows, panels...  65.6 us
    all_gather x1, waiting for transfers between devices, shards(): whole_block = lax.all_gather(final, 'vecs', axis=1, tiled=True)  60.7 us
    pallas_call x8, Pallas kernels, chebyshev_step(): pl.pallas_call(functools.partial(step_kernel, group, len(pieces), kind, e...  58.9 us
    ppermute x4, waiting for transfers between devices, filtered_block(): before = lax.ppermute(high, 'rows', up)  41.1 us
    all_gather x1, waiting for transfers between devices, shards(): gram = lax.all_gather(summed, 'vecs', axis=0, tiled=True)  26.5 us
    ppermute x4, starting transfers between devices, filtered_block(): before = lax.ppermute(high, 'rows', up)  20.7 us
    ppermute x4, waiting for transfers between devices, filtered_block(): after = lax.ppermute(low, 'rows', down)  10.9 us
  transfers between devices with their start and end apart: 11, of which 10 were waited for; matrix products, arithmetic and copies ran while one was open for 1% of the time, Pallas kernels for 7%

profile of v2, /device:TPU:0, one launch (start us, length us, event | category | flops | bytes accessed | tf_op | source)
XLA Modules:
  0.0 415.7 jit_solution(16204966987759582352)
XLA Ops:
  6.5 1.3 fusion.7
  7.8 1.3 collective-permute-start.1
  9.1 5.6 %collective-permute-start = (bf16[1024,256]{1,0:T(8,128)(2,1)S(1)}, bf16[1024,256]{1,0:T(8,128)(2,1)S(1)}, u32[]{:S(2)}, u32[]{:S(2)}) collective-permute-start(bf16[1024,256]{1,0:T(8,128)(2,1)S(1)} %get-tuple-element.30.refs_3_.refs_2_), channel_id=1, source_target_pairs={{0,4},{4,8},{8,12},{12,16},{16,20},{20,24},{24,28},{1,5},{5,9},{9,... | collective-permute-start | bytes 1572872 | tf_op jit(solution)/shard_map/ppermute | solution.py:286
  14.7 2.3 slice.52.refs_2_.refs_1_.refs_4_.refs_5_
  17.2 0.6 add.29.index_ref
  17.8 1.1 pad_maximum_fusion.1.refs_6_.refs_7_
  18.9 5.7 %collective-permute-done.1.refs_4_ = bf16[1024,256]{1,0:T(8,128)(2,1)S(1)} collective-permute-done((bf16[1024,256]{1,0:T(8,128)(2,1)S(1)}, bf16[1024,256]{1,0:T(8,128)(2,1)S(1)}, u32[]{:S(2)}, u32[]{:S(2)}) %collective-permute-start.1) | collective-permute-done | bytes 524320 | tf_op jit(solution)/shard_map/ppermute | solution.py:287
  24.7 11.4 %collective-permute-done.refs_0_ = bf16[1024,256]{1,0:T(8,128)(2,1)S(1)} collective-permute-done((bf16[1024,256]{1,0:T(8,128)(2,1)S(1)}, bf16[1024,256]{1,0:T(8,128)(2,1)S(1)}, u32[]{:S(2)}, u32[]{:S(2)}) %collective-permute-start) | collective-permute-done | bytes 524320 | tf_op jit(solution)/shard_map/ppermute | solution.py:286
  36.1 0.8 copy-done.10
  36.9 7.0 %shard_map.37 = (bf16[2048,256]{1,0:T(8,128)(2,1)}, f32[2048,256]{1,0:T(8,128)}) custom-call(s32[80]{0:T(128)} %add.29.index_ref, bf16[1024,256]{1,0:T(8,128)(2,1)} %copy-done.10, bf16[1024,256]{1,0:T(8,128)(2,1)} %copy-done, bf16[2048,256]{1,0:T(8,128)(2,1)} %slice.52.refs_2_.refs_1_.refs_4_.refs_5_, bf16[1024,256]{1,0:T(8,128)(2,1)} %copy-done.1, ...), custom_call_target="tpu_custom_call" | custom-call | flops 671088640 | bytes 11010048 | tf_op jit(solution)/shard_map/pallas_call | solution.py:80
  43.9 1.3 fusion.11
  45.1 1.3 collective-permute-start.3
  46.4 5.0 %collective-permute-start.2 = (bf16[1024,256]{1,0:T(8,128)(2,1)S(1)}, bf16[1024,256]{1,0:T(8,128)(2,1)S(1)}, u32[]{:S(2)}, u32[]{:S(2)}) collective-permute-start(bf16[1024,256]{1,0:T(8,128)(2,1)S(1)} %get-tuple-element.38.refs_3_.refs_2_), channel_id=1, source_target_pairs={{0,4},{4,8},{8,12},{12,16},{16,20},{20,24},{24,28},{1,5},{5,9},{9,... | collective-permute-start | bytes 1572872 | tf_op jit(solution)/shard_map/ppermute | solution.py:286
  51.7 0.7 reshape.7.index_ref
  52.3 6.9 %shard_map.38 = (bf16[2048,256]{1,0:T(8,128)(2,1)}, f32[2048,256]{1,0:T(8,128)}) custom-call(s32[80]{0:T(128)} %reshape.7.index_ref, bf16[1024,256]{1,0:T(8,128)(2,1)} %copy-done, bf16[2048,256]{1,0:T(8,128)(2,1)} %slice.52.refs_2_.refs_1_.refs_4_.refs_5_, bf16[1024,256]{1,0:T(8,128)(2,1)} %copy-done.1, bf16[32,5,128,128]{3,2,1,0:T(8,128)(2,1)} %refs_3_.7, ...), custom_call_target="tpu_custom_call" | custom-call | flops 671088640 | bytes 11010048 | tf_op jit(solution)/shard_map/pallas_call | solution.py:80
  59.3 2.4 collective-permute-done.3.refs_4_
  61.6 11.4 %collective-permute-done.2.refs_0_ = bf16[1024,256]{1,0:T(8,128)(2,1)S(1)} collective-permute-done((bf16[1024,256]{1,0:T(8,128)(2,1)S(1)}, bf16[1024,256]{1,0:T(8,128)(2,1)S(1)}, u32[]{:S(2)}, u32[]{:S(2)}) %collective-permute-start.2) | collective-permute-done | bytes 524320 | tf_op jit(solution)/shard_map/ppermute | solution.py:286
  73.0 0.8 copy-done.13
  73.9 7.7 %shard_map.39 = (bf16[2048,256]{1,0:T(8,128)(2,1)}, f32[2048,256]{1,0:T(8,128)}) custom-call(s32[80]{0:T(128)} %add.29.index_ref, bf16[1024,256]{1,0:T(8,128)(2,1)} %copy-done.13, bf16[1024,256]{1,0:T(8,128)(2,1)} %copy-done.4, bf16[2048,256]{1,0:T(8,128)(2,1)} %get-tuple-element.18.refs_2_.refs_1_, bf16[1024,256]{1,0:T(8,128)(2,1)} %copy-done.5, ...), custom_call_target="tpu_custom_call" | custom-call | flops 671088640 | bytes 11010048 | tf_op jit(solution)/shard_map/pallas_call | solution.py:80
  81.6 1.3 fusion.10
  82.9 1.3 collective-permute-start.5
  84.2 5.0 %collective-permute-start.4 = (bf16[1024,256]{1,0:T(8,128)(2,1)S(1)}, bf16[1024,256]{1,0:T(8,128)(2,1)S(1)}, u32[]{:S(2)}, u32[]{:S(2)}) collective-permute-start(bf16[1024,256]{1,0:T(8,128)(2,1)S(1)} %get-tuple-element.36.refs_3_.refs_2_), channel_id=1, source_target_pairs={{0,4},{4,8},{8,12},{12,16},{16,20},{20,24},{24,28},{1,5},{5,9},{9,... | collective-permute-start | bytes 1572872 | tf_op jit(solution)/shard_map/ppermute | solution.py:286
  89.2 7.4 %shard_map.40 = (bf16[2048,256]{1,0:T(8,128)(2,1)}, f32[2048,256]{1,0:T(8,128)}) custom-call(s32[80]{0:T(128)} %reshape.7.index_ref, bf16[1024,256]{1,0:T(8,128)(2,1)} %copy-done.4, bf16[2048,256]{1,0:T(8,128)(2,1)} %get-tuple-element.18.refs_2_.refs_1_, bf16[1024,256]{1,0:T(8,128)(2,1)} %copy-done.5, bf16[32,5,128,128]{3,2,1,0:T(8,128)(2,1)} %refs_3_.7, ...), custom_call_target="tpu_custom_call" | custom-call | flops 671088640 | bytes 11010048 | tf_op jit(solution)/shard_map/pallas_call | solution.py:80
  96.6 2.7 collective-permute-done.5.refs_4_
  99.3 11.4 %collective-permute-done.4.refs_0_ = bf16[1024,256]{1,0:T(8,128)(2,1)S(1)} collective-permute-done((bf16[1024,256]{1,0:T(8,128)(2,1)S(1)}, bf16[1024,256]{1,0:T(8,128)(2,1)S(1)}, u32[]{:S(2)}, u32[]{:S(2)}) %collective-permute-start.4) | collective-permute-done | bytes 524320 | tf_op jit(solution)/shard_map/ppermute | solution.py:286
  110.7 0.8 copy-done.14
  111.5 8.0 %shard_map.41 = (bf16[2048,256]{1,0:T(8,128)(2,1)}, f32[2048,256]{1,0:T(8,128)}) custom-call(s32[80]{0:T(128)} %add.29.index_ref, bf16[1024,256]{1,0:T(8,128)(2,1)} %copy-done.14, bf16[1024,256]{1,0:T(8,128)(2,1)} %copy-done.2, bf16[2048,256]{1,0:T(8,128)(2,1)} %get-tuple-element.22.refs_2_.refs_1_, bf16[1024,256]{1,0:T(8,128)(2,1)} %copy-done.3, ...), custom_call_target="tpu_custom_call" | custom-call | flops 671088640 | bytes 11010048 | tf_op jit(solution)/shard_map/pallas_call | solution.py:80
  119.5 1.3 fusion.9
  120.8 1.3 collective-permute-start.7
  122.1 5.0 %collective-permute-start.6 = (bf16[1024,256]{1,0:T(8,128)(2,1)S(1)}, bf16[1024,256]{1,0:T(8,128)(2,1)S(1)}, u32[]{:S(2)}, u32[]{:S(2)}) collective-permute-start(bf16[1024,256]{1,0:T(8,128)(2,1)S(1)} %get-tuple-element.34.refs_3_.refs_2_), channel_id=1, source_target_pairs={{0,4},{4,8},{8,12},{12,16},{16,20},{20,24},{24,28},{1,5},{5,9},{9,... | collective-permute-start | bytes 1572872 | tf_op jit(solution)/shard_map/ppermute | solution.py:286
  127.1 7.5 %shard_map.42 = (bf16[2048,256]{1,0:T(8,128)(2,1)}, f32[2048,256]{1,0:T(8,128)}) custom-call(s32[80]{0:T(128)} %reshape.7.index_ref, bf16[1024,256]{1,0:T(8,128)(2,1)} %copy-done.2, bf16[2048,256]{1,0:T(8,128)(2,1)} %get-tuple-element.22.refs_2_.refs_1_, bf16[1024,256]{1,0:T(8,128)(2,1)} %copy-done.3, bf16[32,5,128,128]{3,2,1,0:T(8,128)(2,1)} %refs_3_.7, ...), custom_call_target="tpu_custom_call" | custom-call | flops 671088640 | bytes 11010048 | tf_op jit(solution)/shard_map/pallas_call | solution.py:80
  134.7 7.0 %shard_map.44 = bf16[2048,256]{1,0:T(8,128)(2,1)} custom-call(s32[80]{0:T(128)} %reshape.7.index_ref, bf16[1024,256]{1,0:T(8,128)(2,1)} %copy-done.6, bf16[2048,256]{1,0:T(8,128)(2,1)} %get-tuple-element.26.refs_2_.refs_1_, bf16[1024,256]{1,0:T(8,128)(2,1)} %copy-done.7, bf16[32,5,128,128]{3,2,1,0:T(8,128)(2,1)} %refs_3_.7, ...), custom_call_target="tpu_custom_call" | custom-call | flops 671088640 | bytes 11010048 | tf_op jit(solution)/shard_map/pallas_call | solution.py:80
  141.7 7.0 %collective-permute-done.6.refs_0_ = bf16[1024,256]{1,0:T(8,128)(2,1)S(1)} collective-permute-done((bf16[1024,256]{1,0:T(8,128)(2,1)S(1)}, bf16[1024,256]{1,0:T(8,128)(2,1)S(1)}, u32[]{:S(2)}, u32[]{:S(2)}) %collective-permute-start.6) | collective-permute-done | bytes 524320 | tf_op jit(solution)/shard_map/ppermute | solution.py:286
  148.7 0.8 copy-done.16
  149.5 7.5 %shard_map.43 = bf16[2048,256]{1,0:T(8,128)(2,1)} custom-call(s32[80]{0:T(128)} %add.29.index_ref, bf16[1024,256]{1,0:T(8,128)(2,1)} %copy-done.16, bf16[1024,256]{1,0:T(8,128)(2,1)} %copy-done.6, bf16[2048,256]{1,0:T(8,128)(2,1)} %get-tuple-element.26.refs_2_.refs_1_, bf16[1024,256]{1,0:T(8,128)(2,1)} %copy-done.7, bf16[1024,256]{1,0:T(8,128)(2,1)} %copy-done.15, ...), custom_call_target="tpu_custom_call" | custom-call | flops 671088640 | bytes 11010048 | tf_op jit(solution)/shard_map/pallas_call | solution.py:80
  157.0 1.3 fusion.8
  158.2 1.5 pad_maximum_fusion
  159.8 60.7 %all-gather.3.cloned.1.call-done = bf16[4096,1024]{1,0:T(8,128)(2,1)} async-done(((bf16[4096,256]{1,0:T(8,128)(2,1)}), bf16[4096,1024]{1,0:T(8,128)(2,1)}) %all-gather.3.cloned.1.call-update) | async-done | bytes 8388624 | tf_op jit(solution)/shard_map/all_gather | solution.py:307
  220.4 6.7 %fusion.6 = f32[256,1024]{0,1:T(8,128)S(1)} fusion(bf16[4096,1024]{1,0:T(8,128)(2,1)} %all-gather.3.cloned.1.call-done, bf16[1024,256]{1,0:T(8,128)(2,1)S(1)} %get-tuple-element.32, bf16[2048,256]{1,0:T(8,128)(2,1)S(1)} %copy-done.8, bf16[1024,256]{1,0:T(8,128)(2,1)S(1)} %get-tuple-element.31), kind=kOutput, calls=%fused_computation.19 | convolution fusion | flops 2153775104 | bytes 11534336 | tf_op jit(solution)/shard_map/dot_general | solution.py:308
  227.2 0.1 fusion.1
  227.3 0.2 fusion
  227.5 0.2 copy.15
  227.8 0.9 pad_maximum_fusion.2
  228.8 73.8 %all-reduce.2.cloned.1.call-done = f32[256,640]{1,0:T(8,128)} async-done(((f32[256,640]{1,0:T(8,128)}), f32[256,640]{1,0:T(8,128)}) %all-reduce.2.cloned.1.call-update) | async-done | bytes 655376 | tf_op jit(solution)/shard_map/psum | solution.py:311
  302.6 26.5 %all-gather.5.cloned.1.call-done.gram_ref = f32[1024,640]{1,0:T(8,128)} async-done(((f32[256,640]{1,0:T(8,128)}), f32[1024,640]{1,0:T(8,128)}) %all-gather.5.cloned.1.call-update) | async-done | bytes 2621456 | tf_op jit(solution)/shard_map/all_gather | solution.py:312
  329.1 65.6 %shard_map.45 = f32[1024,1024]{1,0:T(8,128)} custom-call(f32[1024,640]{1,0:T(8,128)} %all-gather.5.cloned.1.call-done.gram_ref), custom_call_target="tpu_custom_call" | custom-call | flops 42949672960 | bytes 8388608 | tf_op jit(solution)/shard_map/pallas_call | solution.py:231
  394.7 6.1 %fusion.2 = f32[4096,256]{1,0:T(8,128)S(1)} fusion(bf16[4096,1024]{1,0:T(8,128)(2,1)} %all-gather.3.cloned.1.call-done, f32[1024,1024]{1,0:T(8,128)} %shard_map.45, s32[]{:T(128)S(6)} %select_n.21), kind=kOutput, calls=%fused_computation.12 | convolution fusion | flops 2147483648 | bytes 13107204 | tf_op jit(solution)/shard_map/dot_general | solution.py:250
  400.8 8.3 %convolution_add_fusion = f32[4096,256]{1,0:T(8,128)} fusion(f32[4096,256]{1,0:T(8,128)S(1)} %fusion.2, bf16[4096,1024]{1,0:T(8,128)(2,1)} %all-gather.3.cloned.1.call-done, f32[1024,1024]{1,0:T(8,128)} %shard_map.45, s32[]{:T(128)S(6)} %select_n.21), kind=kOutput, calls=%fused_computation | convolution fusion | flops 2149580800 | bytes 17825796 | tf_op jit(solution)/shard_map/dot_general | solution.py:251
  (48 shorter events, 0.7 us)
Async XLA Ops:
  6.5 10.5 %copy-start.17 = (s32[32,5]{0,1:T(8,128)S(1)}, s32[32,5]{0,1:T(8,128)}, u32[]{:S(2)}) copy-start(s32[32,5]{0,1:T(8,128)} %param.5) | copy-start | bytes 1924
  6.5 213.9 %all-gather.3.cloned.1.call-start = ((), (), s32[]{:S(2)}) async-start(), calls=%async_computation | async-start | bytes 10485760 | tf_op jit(solution)/shard_map/all_gather | solution.py:307
  7.8 28.2 %copy-start = (bf16[1024,256]{1,0:T(8,128)(2,1)}, bf16[1024,256]{1,0:T(8,128)(2,1)S(1)}, u32[]{:S(2)}) copy-start(bf16[1024,256]{1,0:T(8,128)(2,1)S(1)} %get-tuple-element.29.refs_1_.refs_0_) | copy-start | bytes 1572868
  7.8 28.2 %copy-start.1 = (bf16[1024,256]{1,0:T(8,128)(2,1)}, bf16[1024,256]{1,0:T(8,128)(2,1)S(1)}, u32[]{:S(2)}) copy-start(bf16[1024,256]{1,0:T(8,128)(2,1)S(1)} %get-tuple-element.30.refs_3_.refs_2_) | copy-start | bytes 1572868
  7.8 16.8 %collective-permute-start.1 = (bf16[1024,256]{1,0:T(8,128)(2,1)S(1)}, bf16[1024,256]{1,0:T(8,128)(2,1)S(1)}, u32[]{:S(2)}, u32[]{:S(2)}) collective-permute-start(bf16[1024,256]{1,0:T(8,128)(2,1)S(1)} %get-tuple-element.29.refs_1_.refs_0_), channel_id=1, source_target_pairs={{4,0},{8,4},{12,8},{16,12},{20,16},{24,20},{28,24},{5,1},{9,5},{13... | collective-permute-start | bytes 1572872 | tf_op jit(solution)/shard_map/ppermute | solution.py:287
  9.1 26.9 %collective-permute-start = (bf16[1024,256]{1,0:T(8,128)(2,1)S(1)}, bf16[1024,256]{1,0:T(8,128)(2,1)S(1)}, u32[]{:S(2)}, u32[]{:S(2)}) collective-permute-start(bf16[1024,256]{1,0:T(8,128)(2,1)S(1)} %get-tuple-element.30.refs_3_.refs_2_), channel_id=1, source_target_pairs={{0,4},{4,8},{8,12},{12,16},{16,20},{20,24},{24,28},{1,5},{5,9},{9,... | collective-permute-start | bytes 1572872 | tf_op jit(solution)/shard_map/ppermute | solution.py:286
  24.7 11.4 %copy-start.9 = (bf16[1024,256]{1,0:T(8,128)(2,1)}, bf16[1024,256]{1,0:T(8,128)(2,1)S(1)}, u32[]{:S(2)}) copy-start(bf16[1024,256]{1,0:T(8,128)(2,1)S(1)} %collective-permute-done.1.refs_4_) | copy-start | bytes 1572868
  36.1 0.8 copy-start.10
  45.1 14.1 %copy-start.4 = (bf16[1024,256]{1,0:T(8,128)(2,1)}, bf16[1024,256]{1,0:T(8,128)(2,1)S(1)}, u32[]{:S(2)}) copy-start(bf16[1024,256]{1,0:T(8,128)(2,1)S(1)} %get-tuple-element.37.refs_1_.refs_0_) | copy-start | bytes 1572868
  45.1 14.1 %copy-start.5 = (bf16[1024,256]{1,0:T(8,128)(2,1)}, bf16[1024,256]{1,0:T(8,128)(2,1)S(1)}, u32[]{:S(2)}) copy-start(bf16[1024,256]{1,0:T(8,128)(2,1)S(1)} %get-tuple-element.38.refs_3_.refs_2_) | copy-start | bytes 1572868
  45.1 16.5 %collective-permute-start.3 = (bf16[1024,256]{1,0:T(8,128)(2,1)S(1)}, bf16[1024,256]{1,0:T(8,128)(2,1)S(1)}, u32[]{:S(2)}, u32[]{:S(2)}) collective-permute-start(bf16[1024,256]{1,0:T(8,128)(2,1)S(1)} %get-tuple-element.37.refs_1_.refs_0_), channel_id=1, source_target_pairs={{4,0},{8,4},{12,8},{16,12},{20,16},{24,20},{28,24},{5,1},{9,5},{13... | collective-permute-start | bytes 1572872 | tf_op jit(solution)/shard_map/ppermute | solution.py:287
  46.4 26.6 %collective-permute-start.2 = (bf16[1024,256]{1,0:T(8,128)(2,1)S(1)}, bf16[1024,256]{1,0:T(8,128)(2,1)S(1)}, u32[]{:S(2)}, u32[]{:S(2)}) collective-permute-start(bf16[1024,256]{1,0:T(8,128)(2,1)S(1)} %get-tuple-element.38.refs_3_.refs_2_), channel_id=1, source_target_pairs={{0,4},{4,8},{8,12},{12,16},{16,20},{20,24},{24,28},{1,5},{5,9},{9,... | collective-permute-start | bytes 1572872 | tf_op jit(solution)/shard_map/ppermute | solution.py:286
  61.6 11.4 %copy-start.11 = (bf16[1024,256]{1,0:T(8,128)(2,1)}, bf16[1024,256]{1,0:T(8,128)(2,1)S(1)}, u32[]{:S(2)}) copy-start(bf16[1024,256]{1,0:T(8,128)(2,1)S(1)} %collective-permute-done.3.refs_4_) | copy-start | bytes 1572868
  73.0 0.8 copy-start.13
  82.8 13.8 %copy-start.2 = (bf16[1024,256]{1,0:T(8,128)(2,1)}, bf16[1024,256]{1,0:T(8,128)(2,1)S(1)}, u32[]{:S(2)}) copy-start(bf16[1024,256]{1,0:T(8,128)(2,1)S(1)} %get-tuple-element.35.refs_1_.refs_0_) | copy-start | bytes 1572868
  82.8 13.8 %copy-start.3 = (bf16[1024,256]{1,0:T(8,128)(2,1)}, bf16[1024,256]{1,0:T(8,128)(2,1)S(1)}, u32[]{:S(2)}) copy-start(bf16[1024,256]{1,0:T(8,128)(2,1)S(1)} %get-tuple-element.36.refs_3_.refs_2_) | copy-start | bytes 1572868
  82.9 16.5 %collective-permute-start.5 = (bf16[1024,256]{1,0:T(8,128)(2,1)S(1)}, bf16[1024,256]{1,0:T(8,128)(2,1)S(1)}, u32[]{:S(2)}, u32[]{:S(2)}) collective-permute-start(bf16[1024,256]{1,0:T(8,128)(2,1)S(1)} %get-tuple-element.35.refs_1_.refs_0_), channel_id=1, source_target_pairs={{4,0},{8,4},{12,8},{16,12},{20,16},{24,20},{28,24},{5,1},{9,5},{13... | collective-permute-start | bytes 1572872 | tf_op jit(solution)/shard_map/ppermute | solution.py:287
  84.2 26.6 %collective-permute-start.4 = (bf16[1024,256]{1,0:T(8,128)(2,1)S(1)}, bf16[1024,256]{1,0:T(8,128)(2,1)S(1)}, u32[]{:S(2)}, u32[]{:S(2)}) collective-permute-start(bf16[1024,256]{1,0:T(8,128)(2,1)S(1)} %get-tuple-element.36.refs_3_.refs_2_), channel_id=1, source_target_pairs={{0,4},{4,8},{8,12},{12,16},{16,20},{20,24},{24,28},{1,5},{5,9},{9,... | collective-permute-start | bytes 1572872 | tf_op jit(solution)/shard_map/ppermute | solution.py:286
  99.3 11.4 %copy-start.12 = (bf16[1024,256]{1,0:T(8,128)(2,1)}, bf16[1024,256]{1,0:T(8,128)(2,1)S(1)}, u32[]{:S(2)}) copy-start(bf16[1024,256]{1,0:T(8,128)(2,1)S(1)} %collective-permute-done.5.refs_4_) | copy-start | bytes 1572868
  110.7 0.8 copy-start.14
  120.8 13.9 %copy-start.6 = (bf16[1024,256]{1,0:T(8,128)(2,1)}, bf16[1024,256]{1,0:T(8,128)(2,1)S(1)}, u32[]{:S(2)}) copy-start(bf16[1024,256]{1,0:T(8,128)(2,1)S(1)} %get-tuple-element.33.refs_1_.refs_0_) | copy-start | bytes 1572868
  120.8 13.9 %copy-start.7 = (bf16[1024,256]{1,0:T(8,128)(2,1)}, bf16[1024,256]{1,0:T(8,128)(2,1)S(1)}, u32[]{:S(2)}) copy-start(bf16[1024,256]{1,0:T(8,128)(2,1)S(1)} %get-tuple-element.34.refs_3_.refs_2_) | copy-start | bytes 1572868
  120.8 20.9 %collective-permute-start.7 = (bf16[1024,256]{1,0:T(8,128)(2,1)S(1)}, bf16[1024,256]{1,0:T(8,128)(2,1)S(1)}, u32[]{:S(2)}, u32[]{:S(2)}) collective-permute-start(bf16[1024,256]{1,0:T(8,128)(2,1)S(1)} %get-tuple-element.33.refs_1_.refs_0_), channel_id=1, source_target_pairs={{4,0},{8,4},{12,8},{16,12},{20,16},{24,20},{28,24},{5,1},{9,5},{13... | collective-permute-start | bytes 1572872 | tf_op jit(solution)/shard_map/ppermute | solution.py:287
  122.1 26.6 %collective-permute-start.6 = (bf16[1024,256]{1,0:T(8,128)(2,1)S(1)}, bf16[1024,256]{1,0:T(8,128)(2,1)S(1)}, u32[]{:S(2)}, u32[]{:S(2)}) collective-permute-start(bf16[1024,256]{1,0:T(8,128)(2,1)S(1)} %get-tuple-element.34.refs_3_.refs_2_), channel_id=1, source_target_pairs={{0,4},{4,8},{8,12},{12,16},{16,20},{20,24},{24,28},{1,5},{5,9},{9,... | collective-permute-start | bytes 1572872 | tf_op jit(solution)/shard_map/ppermute | solution.py:286
  141.7 7.0 %copy-start.15 = (bf16[1024,256]{1,0:T(8,128)(2,1)}, bf16[1024,256]{1,0:T(8,128)(2,1)S(1)}, u32[]{:S(2)}) copy-start(bf16[1024,256]{1,0:T(8,128)(2,1)S(1)} %collective-permute-done.7.refs_4_) | copy-start | bytes 1572868
  148.7 0.8 copy-start.16
  149.5 8.8 %copy-start.8 = (bf16[2048,256]{1,0:T(8,128)(2,1)S(1)}, bf16[2048,256]{1,0:T(8,128)(2,1)}, u32[]{:S(2)}) copy-start(bf16[2048,256]{1,0:T(8,128)(2,1)} %shard_map.44) | copy-start | bytes 3145732
  159.7 142.9 %all-reduce.2.cloned.1.call-start = ((), (), s32[]{:S(2)}) async-start(), calls=%async_computation.1 | async-start | bytes 1310720 | tf_op jit(solution)/shard_map/psum | solution.py:311
  228.8 100.3 %all-gather.5.cloned.1.call-start = ((), (), s32[]{:S(2)}) async-start(), calls=%async_computation.2 | async-start | bytes 3276800 | tf_op jit(solution)/shard_map/all_gather | solution.py:312
Sparse Core Ops, SparseCore 0:
  159.8 60.5 all-gather.2
  228.9 73.6 all-reduce.1
  304.2 24.8 all-gather.4
